TPU v7x, 512 devices: a whole 4x4x16 slice. The times are simulated.
512 devices in a mesh: probe: 16 (over y, x), space: 32 (over z, core).
Axes of the slice: x: 4, y: 4, z: 16, core: 2. Of those that a mesh axis runs over, the one named last changes fastest.
Arguments:
- probes: float32 [128, 131072], P('probe', 'space'), may hold values from -6 to 6
- sensitivity: float32 [8, 8, 65536], P(None, None, 'space'), may hold values from -2.1 to 2.1
- obs_weight: float32 [8, 65536], P(None, 'space'), may hold values from 0.5 to 4
- prior_weight: float32 [131072], P('space'), may hold values from 0.2 to 2
- connectivity: int32 [8, 65536], P(None, 'space'), may hold values from 0 to 4351, as said below
Outputs:
- basis: float32 [128, 131072], P('probe', 'space')
- factor: float32 [128, 128], replicated
Inputs may be any that keep to these rules, and one draw needn't show every extreme that they name: Each column holds 8 distinct numbers. For an element of the block of device d of space (columns d * 2048 to (d + 1) * 2048 - 1), connectivity + d * 4096 - 128 is an existing node, and the values 0 and 4351 are both named wherever those nodes exist.
All inputs are finite; a program needn't handle non-finite values.
Results may differ from a plain program's by a relative error of at most 0.0003.
Values sent between devices are 32-bit elements; how exact they have to be, the bound alone decides.
No kernel may reach another device: no remote copies, remote signals or barrier semaphores. Data moves between devices by JAX's collectives and lax.ppermute only.
A program may use at most 64 MiB of HBM per device.

v0:
```python
import math

import jax
import jax.numpy as jnp
from jax import lax
from jax.sharding import PartitionSpec as P

HALO = 128


highest = lax.Precision.HIGHEST


def extended_2(block, sides, width):
    for axis, dim in sides:
        count = lax.axis_size(axis)
        forward = [(i, i + 1) for i in range(count - 1)]
        backward = [(target, source) for source, target in forward]
        low = lax.ppermute(
            lax.slice_in_dim(block, block.shape[dim] - width, None, axis=dim), axis, forward
        )
        high = lax.ppermute(lax.slice_in_dim(block, 0, width, axis=dim), axis, backward)
        block = jnp.concatenate([low, block, high], axis=dim)
    return block


def shifted(block, axis, distance):
    devices = range(lax.axis_size(axis))
    route = [(i - distance, i) for i in devices if i - distance in devices]
    return lax.ppermute(block, axis, route)


def element_images(extended, sensitivity, obs_weight, local):
    gathered = extended[:, local]
    gauss_count = sensitivity.shape[0]
    corner_count = sensitivity.shape[1]
    observed = []
    for gauss in range(gauss_count):
        total = gathered[:, 0, :] * sensitivity[gauss, 0][None, :]
        for corner in range(1, corner_count):
            total = total + gathered[:, corner, :] * sensitivity[gauss, corner][None, :]
        observed.append(total * obs_weight[gauss][None, :])
    pulled = []
    for corner in range(corner_count):
        total = observed[0] * sensitivity[0, corner][None, :]
        for gauss in range(1, gauss_count):
            total = total + observed[gauss] * sensitivity[gauss, corner][None, :]
        pulled.append(total)
    pulled = jnp.stack(pulled, axis=1)
    return jnp.zeros(extended.shape, jnp.float32).at[:, local].add(pulled)


def gram_over_space(partial_value):
    return lax.psum(partial_value, "space")


def orthonormal(rows, reduce_gram):
    gram_first = reduce_gram(
        jnp.dot(rows, rows.T, precision=highest, preferred_element_type=jnp.float32)
    )
    lower_first = jnp.linalg.cholesky(gram_first)
    basis_first = lax.linalg.triangular_solve(lower_first, rows, left_side=True, lower=True)
    gram_second = reduce_gram(
        jnp.dot(basis_first, basis_first.T, precision=highest, preferred_element_type=jnp.float32)
    )
    lower_second = jnp.linalg.cholesky(gram_second)
    basis = lax.linalg.triangular_solve(lower_second, basis_first, left_side=True, lower=True)
    factor = jnp.dot(
        lower_first, lower_second, precision=highest, preferred_element_type=jnp.float32
    ).T
    return (basis, factor)


def on_device(probes, sensitivity, obs_weight, prior_weight, connectivity):
    node_count = probes.shape[1]
    probe_count = probes.shape[0]
    extended = extended_2(probes, (("space", 1),), HALO)
    summed = element_images(extended, sensitivity, obs_weight, connectivity)
    lower_rim = shifted(summed[:, :HALO], "space", -1)
    upper_rim = shifted(summed[:, HALO + node_count :], "space", 1)
    images = summed[:, HALO : HALO + node_count] + prior_weight[None, :] * probes
    images = images.at[:, node_count - HALO :].add(lower_rim)
    images = images.at[:, :HALO].add(upper_rim)
    scale = math.sqrt(float(node_count * lax.axis_size("space")))
    whole = lax.all_gather(images, "probe", axis=0, tiled=True)
    basis, factor = orthonormal(whole, gram_over_space)
    basis = lax.dynamic_slice_in_dim(basis, lax.axis_index("probe") * probe_count, probe_count, 0)
    return (basis * scale, factor / scale)


def solution(mesh):
    return jax.shard_map(
        on_device,
        mesh=mesh,
        in_specs=(
            P("probe", "space"),
            P(None, None, "space"),
            P(None, "space"),
            P("space"),
            P(None, "space"),
        ),
        out_specs=(P("probe", "space"), P()),
        check_vma=False,
    )
```

profile of v0, /device:TPU:1, one launch (start us, length us, event | category | flops | bytes accessed | tf_op | source)
XLA Modules:
  0.0 697.5 jit_solution(16327532529719816883)
XLA Ops:
  7.2 0.7 fusion.30
  7.9 4.9 collective-permute-start
  12.8 5.1 collective-permute-start.1
  18.0 1.7 fusion.28
  19.7 1.7 fusion.27
  21.4 1.9 fusion.26
  23.3 1.3 fusion.31
  24.5 0.9 fusion.2
  25.4 1.2 fusion.29
  26.6 0.6 compare_reduce_fusion.2
  27.2 0.9 pad_maximum_fusion
  28.2 0.6 copy.43
  28.8 54.8 %gather_fusion = f32[16384,8]{1,0:T(8,128)} fusion(f32[8,4352]{0,1:T(8,128)S(1)} %copy.43, s32[16384]{0:T(1024)S(1)} %broadcast_clamp_fusion), kind=kCustom, calls=%fused_computation | custom fusion | bytes 1114112 | tf_op jit(solution)/shard_map/gather | solution.py:34
  83.6 5.5 copy.44
  89.1 0.6 multiply_add_fusion.1
  90.0 0.1 multiply_add_fusion.6
  90.9 0.8 stack.2
  91.7 4.6 copy.63
  96.3 88.2 %scatter_custom_fusion = f32[8,4352]{0,1:T(8,128)S(1)} fusion(s32[16384]{0:T(1024)S(1)} %bitcast.108, f32[16384,8]{1,0:T(8,128)} %bitcast.104, f32[]{:T(128)} %constant.95.clone.1), kind=kCustom, calls=%fused_computation.3 | custom fusion | flops 131072 | bytes 139776 | tf_op jit(solution)/shard_map/scatter-add | solution.py:50
  184.4 1.5 slice.540
  185.9 2.2 copy.64
  188.2 1.9 collective-permute-start.2
  190.2 3.7 collective-permute-start.3
  193.9 0.7 collective-permute-done.3
  194.6 0.6 fusion.21
  195.2 0.6 copy-done.1
  195.9 62.5 %all-gather.2.cloned.1.call-done = f32[128,4096]{1,0:T(8,128)} async-done(((f32[8,4096]{1,0:T(8,128)}), f32[128,4096]{1,0:T(8,128)}) %all-gather.2.cloned.1.call-update) | async-done | bytes 2097168 | tf_op jit(solution)/shard_map/all_gather | solution.py:85
  258.5 4.7 fusion.32
  263.2 0.2 all-reduce.5.cloned.1.call-start
  263.4 187.4 %all-reduce.3.cloned.1.call-done = f32[128,128]{0,1:T(8,128)} async-done(((f32[128,128]{0,1:T(8,128)}), f32[128,128]{0,1:T(8,128)}) %all-reduce.3.cloned.1.call-update) | async-done | bytes 65552 | tf_op jit(solution)/shard_map/psum | solution.py:54
  450.9 0.9 copy.58
  451.8 0.9 fusion.8
  452.6 11.7 %cholesky.44 = f32[128,128]{1,0:T(8,128)S(1)} custom-call(f32[128,128]{1,0:T(8,128)S(1)} %fusion.8), custom_call_target="Cholesky" | custom-call | tf_op jit(solution)/shard_map/jit(cholesky)/cholesky | solution.py:61
  464.4 0.6 compare_reduce_fusion.1
  465.0 0.7 fusion.12
  465.7 9.8 %custom-call.6 = f32[1,128,128]{1,2,0:T(8,128)S(1)} custom-call(f32[1,128,128]{2,1,0:T(8,128)S(1)} %fusion.12), custom_call_target="InvertDiagBlocksLowerTriangular" | custom-call | tf_op jit(solution)/shard_map/triangular_solve/custom-call.0 | solution.py:62
  475.5 3.5 fusion.6
  479.0 2.4 fusion.33
  481.5 179.9 %all-reduce.5.cloned.1.call-done = f32[128,128]{0,1:T(8,128)} async-done(((f32[128,128]{0,1:T(8,128)}), f32[128,128]{0,1:T(8,128)}) %all-reduce.5.cloned.1.call-update) | async-done | bytes 65552 | tf_op jit(solution)/shard_map/psum | solution.py:54
  661.4 0.9 copy.60
  662.3 0.9 fusion.5
  663.2 11.9 %cholesky.55 = f32[128,128]{1,0:T(8,128)S(1)} custom-call(f32[128,128]{1,0:T(8,128)S(1)} %fusion.5), custom_call_target="Cholesky" | custom-call | tf_op jit(solution)/shard_map/jit(cholesky)/cholesky | solution.py:66
  675.2 0.6 compare_reduce_fusion
  675.8 2.1 convolution_multiply_fusion
  677.9 0.6 select_bitcast_fusion
  678.5 9.8 %custom-call.7 = f32[1,128,128]{1,2,0:T(8,128)S(1)} custom-call(f32[1,128,128]{2,1,0:T(8,128)S(1)} %select_bitcast_fusion), custom_call_target="InvertDiagBlocksLowerTriangular" | custom-call | tf_op jit(solution)/shard_map/triangular_solve/custom-call.0 | solution.py:67
  688.3 1.9 fusion.3
  690.2 0.7 dynamic-slice_multiply_fusion
  (36 shorter events, 1.4 us)
Async XLA Ops:
  7.2 251.3 %all-gather.2.cloned.1.call-start = ((), (), s32[]{:S(2)}) async-start(), calls=%async_computation | async-start | bytes 2228224 | tf_op jit(solution)/shard_map/all_gather | solution.py:85
  7.9 19.3 %collective-permute-start = (f32[8,128]{1,0:T(8,128)S(1)}, f32[8,128]{1,0:T(8,128)S(1)}, u32[]{:S(2)}, u32[]{:S(2)}) collective-permute-start(f32[8,128]{1,0:T(8,128)S(1)} %get-tuple-element.103), channel_id=1, source_target_pairs={{0,1},{1,2},{2,3},{3,4},{4,5},{5,6},{6,7},{7,8},{8,9},{9,10},{10,1... | collective-permute-start | bytes 12296 | tf_op jit(solution)/shard_map/ppermute | solution.py:19
  12.8 14.4 %collective-permute-start.1 = (f32[8,128]{1,0:T(8,128)S(1)}, f32[8,128]{1,0:T(8,128)S(1)}, u32[]{:S(2)}, u32[]{:S(2)}) collective-permute-start(f32[8,128]{1,0:T(8,128)S(1)} %get-tuple-element.104), channel_id=1, source_target_pairs={{1,0},{2,1},{3,2},{4,3},{5,4},{6,5},{7,6},{8,7},{9,8},{10,9},{11,1... | collective-permute-start | bytes 12296 | tf_op jit(solution)/shard_map/ppermute | solution.py:22
  185.9 7.9 %copy-start = (f32[8,4096]{1,0:T(8,128)S(1)}, f32[8,4096]{1,0:T(8,128)}, u32[]{:S(2)}) copy-start(f32[8,4096]{1,0:T(8,128)} %param.12) | copy-start | bytes 393220
  185.9 7.9 %copy-start.2 = (f32[4096]{0:T(1024)S(1)}, f32[4096]{0:T(1024)}, u32[]{:S(2)}) copy-start(f32[4096]{0:T(1024)} %param.15) | copy-start | bytes 49156
  188.2 5.7 collective-permute-start.2
  190.2 4.4 collective-permute-start.3
  195.2 0.7 copy-start.1
  195.9 255.0 %all-reduce.3.cloned.1.call-start = ((), (), s32[]{:S(2)}) async-start(), calls=%async_computation.1 | async-start | bytes 131072 | tf_op jit(solution)/shard_map/psum | solution.py:54
  263.2 398.2 %all-reduce.5.cloned.1.call-start = ((), (), s32[]{:S(2)}) async-start(), calls=%async_computation.2 | async-start | bytes 131072 | tf_op jit(solution)/shard_map/psum | solution.py:54
Sparse Core Ops, SparseCore 0:
  196.0 62.4 all-gather.1
  263.3 187.4 all-reduce.2
  481.6 179.7 all-reduce.4
where the time goes:
time: 698 us; the launch traced here: 697 us
  waiting for transfers between devices  431 us (62%)
  other arithmetic  141 us (20%)
  local copies, waits for them, and re-layouts  81.6 us (12%)
  starting transfers between devices  15.9 us (2%)
  matrix products  14.7 us (2%)
  between operations  14.1 us (2%)
    psum x2, waiting for transfers between devices, gram_over_space(): return lax.psum(partial_value, 'space')  367 us
    scatter-add x1, other arithmetic, element_images(): return jnp.zeros(extended.shape, jnp.float32).at[:, local].add(pulled)  88.2 us
    all_gather x1, waiting for transfers between devices, on_device(): whole = lax.all_gather(images, 'probe', axis=0, tiled=True)  62.5 us
    gather x2, local copies, waits for them, and re-layouts, element_images(): gathered = extended[:, local]  60.3 us
  transfers between devices with their start and end apart: 7, of which 4 were waited for; matrix products, arithmetic and copies ran while one was open for 1% of the time, Pallas kernels for 0%

commit v1 on v0

v1 whole, which is shorter than its diff:
```python
import math

import jax
import jax.numpy as jnp
from jax import lax
from jax.experimental import pallas as pl
from jax.experimental.pallas import tpu as pltpu
from jax.sharding import PartitionSpec as P

HALO = 128
LANES = 128
WIDE = 256

highest = lax.Precision.HIGHEST


def shifted(block, axis, distance):
    devices = range(lax.axis_size(axis))
    route = [(i - distance, i) for i in devices if i - distance in devices]
    return lax.ppermute(block, axis, route)


def element_kernel(
    low_ref, probes_ref, high_ref, connectivity_ref, sensitivity_ref, weight_ref, prior_ref,
    images_ref, lower_ref, upper_ref, left_ref, right_ref, total_ref,
):
    probe_count, node_count = probes_ref.shape
    corner_count, element_count = connectivity_ref.shape
    gauss_count = sensitivity_ref.shape[0]
    tiles = node_count // LANES + 2
    blocks = tiles * LANES // WIDE
    rows = total_ref.shape[0]

    def tile(k):
        if k == 0:
            return low_ref[...]
        if k == tiles - 1:
            return high_ref[...]
        return probes_ref[:, (k - 1) * LANES : k * LANES]

    total_ref[...] = jnp.zeros_like(total_ref)

    def chunk(step, carry):
        columns = pl.ds(pl.multiple_of(step * LANES, LANES), LANES)
        gathered = []
        nodes = []
        for corner in range(corner_count):
            node = jnp.broadcast_to(
                connectivity_ref[corner : corner + 1, columns], (probe_count, LANES)
            )
            nodes.append(node)
            lane = node & (LANES - 1)
            place = lax.shift_right_logical(node, 7)
            value = jnp.zeros((probe_count, LANES), jnp.float32)
            for k in range(tiles):
                picked = jnp.take_along_axis(tile(k), lane, axis=1, mode="promise_in_bounds")
                value = jnp.where(place == k, picked, value)
            gathered.append(value)
        observed = []
        for gauss in range(gauss_count):
            value = gathered[0] * sensitivity_ref[gauss, 0:1, columns]
            for corner in range(1, corner_count):
                value = value + gathered[corner] * sensitivity_ref[gauss, corner : corner + 1, columns]
            observed.append(value * weight_ref[gauss : gauss + 1, columns])
        for corner in range(corner_count):
            value = observed[0] * sensitivity_ref[0, corner : corner + 1, columns]
            for gauss in range(1, gauss_count):
                value = value + observed[gauss] * sensitivity_ref[gauss, corner : corner + 1, columns]
            first = value.astype(jnp.bfloat16).astype(jnp.float32)
            rest = value - first
            second = rest.astype(jnp.bfloat16).astype(jnp.float32)
            third = rest - second
            node = nodes[corner]
            place = lax.shift_right_logical(node, 8)
            zero = jnp.zeros_like(value)
            pieces = []
            for k in range(blocks):
                here = place == k
                for piece in (first, second, third):
                    pieces.append(jnp.where(here, piece, zero))
            while len(pieces) * probe_count < rows:
                pieces.append(zero)
            span = slice(corner * LANES, (corner + 1) * LANES)
            left_ref[:, span] = jnp.concatenate(pieces, axis=0).astype(jnp.bfloat16)
            lane = jnp.broadcast_to(node[0:1, :] & (WIDE - 1), (WIDE, LANES))
            row = lax.broadcasted_iota(jnp.int32, (WIDE, LANES), 0)
            right_ref[:, span] = jnp.where(row == lane, 1.0, 0.0).astype(jnp.bfloat16)
        total_ref[...] += lax.dot_general(
            left_ref[...], right_ref[...], (((1,), (1,)), ((), ())),
            preferred_element_type=jnp.float32,
        )
        return carry

    lax.fori_loop(0, element_count // LANES, chunk, 0)

    for block in range(blocks):
        at = block * 3 * probe_count
        value = total_ref[at + 2 * probe_count : at + 3 * probe_count, :]
        value = value + total_ref[at + probe_count : at + 2 * probe_count, :]
        value = value + total_ref[at : at + probe_count, :]
        for half in range(WIDE // LANES):
            k = block * (WIDE // LANES) + half
            part = value[:, half * LANES : (half + 1) * LANES]
            if k == 0:
                lower_ref[...] = part
            elif k == tiles - 1:
                upper_ref[...] = part
            else:
                span = slice((k - 1) * LANES, k * LANES)
                images_ref[:, span] = part + prior_ref[:, span] * probes_ref[:, span]


def element_images(low, probes, high, connectivity, sensitivity, obs_weight, prior_weight):
    probe_count, node_count = probes.shape
    corner_count = connectivity.shape[0]
    blocks = (node_count + 2 * HALO) // WIDE
    rows = -(-blocks * 3 * probe_count // 16) * 16
    vmem = pl.BlockSpec(memory_space=pltpu.VMEM)
    rim = jax.ShapeDtypeStruct((probe_count, HALO), jnp.float32)
    return pl.pallas_call(
        element_kernel,
        out_shape=(jax.ShapeDtypeStruct(probes.shape, jnp.float32), rim, rim),
        in_specs=[vmem] * 7,
        out_specs=(vmem, vmem, vmem),
        scratch_shapes=[
            pltpu.VMEM((rows, corner_count * LANES), jnp.bfloat16),
            pltpu.VMEM((WIDE, corner_count * LANES), jnp.bfloat16),
            pltpu.VMEM((rows, WIDE), jnp.float32),
        ],
        name="element_images",
    )(low, probes, high, connectivity, sensitivity, obs_weight, prior_weight.reshape(1, -1))


def gram_over_space(partial_value):
    return lax.psum(partial_value, "space")


def orthonormal(rows, reduce_gram):
    gram_first = reduce_gram(
        jnp.dot(rows, rows.T, precision=highest, preferred_element_type=jnp.float32)
    )
    lower_first = jnp.linalg.cholesky(gram_first)
    basis_first = lax.linalg.triangular_solve(lower_first, rows, left_side=True, lower=True)
    gram_second = reduce_gram(
        jnp.dot(basis_first, basis_first.T, precision=highest, preferred_element_type=jnp.float32)
    )
    lower_second = jnp.linalg.cholesky(gram_second)
    basis = lax.linalg.triangular_solve(lower_second, basis_first, left_side=True, lower=True)
    factor = jnp.dot(
        lower_first, lower_second, precision=highest, preferred_element_type=jnp.float32
    ).T
    return (basis, factor)


def on_device(probes, sensitivity, obs_weight, prior_weight, connectivity):
    node_count = probes.shape[1]
    probe_count = probes.shape[0]
    low = shifted(probes[:, node_count - HALO :], "space", 1)
    high = shifted(probes[:, :HALO], "space", -1)
    images, lower, upper = element_images(
        low, probes, high, connectivity, sensitivity, obs_weight, prior_weight
    )
    lower_rim = shifted(lower, "space", -1)
    upper_rim = shifted(upper, "space", 1)
    images = images.at[:, node_count - HALO :].add(lower_rim)
    images = images.at[:, :HALO].add(upper_rim)
    scale = math.sqrt(float(node_count * lax.axis_size("space")))
    whole = lax.all_gather(images, "probe", axis=0, tiled=True)
    basis, factor = orthonormal(whole, gram_over_space)
    basis = lax.dynamic_slice_in_dim(basis, lax.axis_index("probe") * probe_count, probe_count, 0)
    return (basis * scale, factor / scale)


def solution(mesh):
    return jax.shard_map(
        on_device,
        mesh=mesh,
        in_specs=(
            P("probe", "space"),
            P(None, None, "space"),
            P(None, "space"),
            P("space"),
            P(None, "space"),
        ),
        out_specs=(P("probe", "space"), P()),
        check_vma=False,
    )
```

time: 698 us -> 556 us (0.80)
  other arithmetic: 141 us -> 52.3 us
  local copies, waits for them, and re-layouts: 81.6 us -> 3.16 us
  Pallas kernels: 0 us -> 21 us
    scatter-add x1 -> x0, other arithmetic: 88.2 us -> none  [element_images(): return jnp.zeros(extended.shape, jnp.float32).at[:, local].add(pulled)]
    gather x2 -> x0, local copies, waits for them, and re-layouts: 60.3 us -> none  [element_images(): gathered = extended[:, local]]
    pallas_call x0 -> x1, Pallas kernels: none -> 21 us  [element_images(): pl.pallas_call(element_kernel, out_shape=(jax.ShapeDtypeStruct(probes.sha...]
    ppermute x2 -> x0, starting transfers between devices: 10 us -> none  [the longest x1 5.11 us: extended_2(): lax.ppermute(lax.slice_in_dim(block, 0, width, axis=dim), axis, backward)]
    ppermute x2 -> x4, starting transfers between devices: 5.59 us -> 15.6 us  [shifted(): return lax.ppermute(block, axis, route)]
    slice x8 -> x1, local copies, waits for them, and re-layouts: 9.94 us -> 0.71 us  [on_device(): high = shifted(probes[:, :HALO], 'space', -1)]
  transfers between devices with their start and end apart: 7 -> 7, of which waited for: 4 -> 4; matrix products, arithmetic and copies ran while one was open for 1% -> 0% of each run, Pallas kernels for 0% -> 0%
where the time goes in v1:
time: 556 us; the launch traced here: 555 us
  waiting for transfers between devices  434 us (78%)
  other arithmetic  52.3 us (9%)
  Pallas kernels  21 us (4%)
  starting transfers between devices  15.9 us (3%)
  matrix products  14.8 us (3%)
  between operations  13.9 us (2%)
    psum x2, waiting for transfers between devices, gram_over_space(): return lax.psum(partial_value, 'space')  368 us
    all_gather x1, waiting for transfers between devices, on_device(): whole = lax.all_gather(images, 'probe', axis=0, tiled=True)  65.6 us
    pallas_call x1, Pallas kernels, element_images(): pl.pallas_call(element_kernel, out_shape=(jax.ShapeDtypeStruct(probes.sha...  21 us
    ppermute x4, starting transfers between devices, shifted(): return lax.ppermute(block, axis, route)  15.6 us
    another operation x3, other arithmetic, orthonormal(): lower_second = jnp.linalg.cholesky(gram_second)  12.7 us
    another operation x3, other arithmetic, orthonormal(): lower_first = jnp.linalg.cholesky(gram_first)  12.4 us
  transfers between devices with their start and end apart: 7, of which 4 were waited for; matrix products, arithmetic and copies ran while one was open for 0% of the time, Pallas kernels for 0%

profile of v1, /device:TPU:1, one launch (start us, length us, event | category | flops | bytes accessed | tf_op | source)
XLA Modules:
  0.0 555.0 jit_solution(12196813496321397394)
XLA Ops:
  7.2 0.0 all-gather.2.cloned.1.call-start
  7.2 0.7 fusion.21
  7.9 4.9 collective-permute-start
  12.8 5.1 collective-permute-start.1
  18.0 0.0 collective-permute-done.low_ref
  18.0 0.0 copy-start
  18.0 0.8 collective-permute-done.1.high_ref
  18.8 0.0 copy-start.1
  18.8 0.0 copy-done
  18.8 0.6 copy-done.1
  19.4 21.0 %element_images.1 = (f32[8,4096]{1,0:T(8,128)}, f32[8,128]{1,0:T(8,128)}, f32[8,128]{1,0:T(8,128)}) custom-call(f32[8,128]{1,0:T(8,128)} %copy-done, f32[8,4096]{1,0:T(8,128)} %probes_ref.1, f32[8,128]{1,0:T(8,128)} %copy-done.1, s32[8,2048]{1,0:T(8,128)} %connectivity_ref.1, f32[8,8,2048]{2,1,0:T(8,128)} %sensitivity_ref.1, f32[8,2048]{1,0:T(8,128)} %weight_ref.1, ...), custom_call_target="tpu_custom_call" | custom-call | tf_op jit(solution)/shard_map/element_images/pallas_call | solution.py:120
  40.3 2.2 collective-permute-start.2
  42.6 0.6 compare_reduce_fusion.2
  43.2 3.3 collective-permute-start.3
  46.5 0.0 collective-permute-done.2
  46.5 1.3 add_dynamic-update-slice_fusion
  47.8 0.0 collective-permute-done.3
  47.8 1.9 fusion.18
  49.7 0.0 all-gather.2.cloned.1.call-update
  49.8 0.0 all-reduce.3.cloned.1.call-start
  49.8 65.6 %all-gather.2.cloned.1.call-done = f32[128,4096]{1,0:T(8,128)} async-done(((f32[8,4096]{1,0:T(8,128)}), f32[128,4096]{1,0:T(8,128)}) %all-gather.2.cloned.1.call-update) | async-done | bytes 2097168 | tf_op jit(solution)/shard_map/all_gather | solution.py:168
  115.4 4.7 fusion.22
  120.1 0.0 all-reduce.3.cloned.1.call-update
  120.1 0.2 all-reduce.5.cloned.1.call-start
  120.3 187.4 %all-reduce.3.cloned.1.call-done = f32[128,128]{0,1:T(8,128)} async-done(((f32[128,128]{0,1:T(8,128)}), f32[128,128]{0,1:T(8,128)}) %all-reduce.3.cloned.1.call-update) | async-done | bytes 65552 | tf_op jit(solution)/shard_map/psum | solution.py:135
  307.8 0.9 copy.8
  308.7 0.9 fusion.5
  309.6 11.7 %cholesky.44 = f32[128,128]{1,0:T(8,128)S(1)} custom-call(f32[128,128]{1,0:T(8,128)S(1)} %fusion.5), custom_call_target="Cholesky" | custom-call | tf_op jit(solution)/shard_map/jit(cholesky)/cholesky | solution.py:142
  321.3 0.6 compare_reduce_fusion.1
  321.9 0.7 fusion.9
  322.6 9.8 %custom-call.6 = f32[1,128,128]{1,2,0:T(8,128)S(1)} custom-call(f32[1,128,128]{2,1,0:T(8,128)S(1)} %fusion.9), custom_call_target="InvertDiagBlocksLowerTriangular" | custom-call | tf_op jit(solution)/shard_map/triangular_solve/custom-call.0 | solution.py:143
  332.4 3.5 fusion.3
  335.9 2.4 fusion.23
  338.3 0.0 all-reduce.5.cloned.1.call-update
  338.4 180.2 %all-reduce.5.cloned.1.call-done = f32[128,128]{0,1:T(8,128)} async-done(((f32[128,128]{0,1:T(8,128)}), f32[128,128]{0,1:T(8,128)}) %all-reduce.5.cloned.1.call-update) | async-done | bytes 65552 | tf_op jit(solution)/shard_map/psum | solution.py:135
  518.6 0.9 copy.10
  519.5 0.9 fusion.2
  520.4 11.9 %cholesky.55 = f32[128,128]{1,0:T(8,128)S(1)} custom-call(f32[128,128]{1,0:T(8,128)S(1)} %fusion.2), custom_call_target="Cholesky" | custom-call | tf_op jit(solution)/shard_map/jit(cholesky)/cholesky | solution.py:147
  532.3 0.7 compare_reduce_fusion
  533.0 2.3 convolution_multiply_fusion
  535.3 0.7 select_bitcast_fusion
  536.0 9.8 %custom-call.7 = f32[1,128,128]{1,2,0:T(8,128)S(1)} custom-call(f32[1,128,128]{2,1,0:T(8,128)S(1)} %select_bitcast_fusion), custom_call_target="InvertDiagBlocksLowerTriangular" | custom-call | tf_op jit(solution)/shard_map/triangular_solve/custom-call.0 | solution.py:148
  545.8 1.9 fusion
  547.8 0.7 dynamic-slice_multiply_fusion
  (2 shorter events, 0.1 us)
Async XLA Ops:
  7.2 108.2 %all-gather.2.cloned.1.call-start = ((), (), s32[]{:S(2)}) async-start(), calls=%async_computation | async-start | bytes 2228224 | tf_op jit(solution)/shard_map/all_gather | solution.py:168
  7.9 10.0 %collective-permute-start = (f32[8,128]{1,0:T(8,128)S(1)}, f32[8,128]{1,0:T(8,128)S(1)}, u32[]{:S(2)}, u32[]{:S(2)}) collective-permute-start(f32[8,128]{1,0:T(8,128)S(1)} %get-tuple-element.35), channel_id=1, source_target_pairs={{0,1},{1,2},{2,3},{3,4},{4,5},{5,6},{6,7},{7,8},{8,9},{9,10},{10,1... | collective-permute-start | bytes 12296 | tf_op jit(solution)/shard_map/ppermute | solution.py:20
  12.8 5.9 %collective-permute-start.1 = (f32[8,128]{1,0:T(8,128)S(1)}, f32[8,128]{1,0:T(8,128)S(1)}, u32[]{:S(2)}, u32[]{:S(2)}) collective-permute-start(f32[8,128]{1,0:T(8,128)S(1)} %get-tuple-element.34), channel_id=1, source_target_pairs={{1,0},{2,1},{3,2},{4,3},{5,4},{6,5},{7,6},{8,7},{9,8},{10,9},{11,1... | collective-permute-start | bytes 12296 | tf_op jit(solution)/shard_map/ppermute | solution.py:20
  18.0 0.8 copy-start
  18.8 0.6 copy-start.1
  40.3 6.2 %collective-permute-start.2 = (f32[8,128]{1,0:T(8,128)}, f32[8,128]{1,0:T(8,128)S(1)}, u32[]{:S(2)}, u32[]{:S(2)}) collective-permute-start(f32[8,128]{1,0:T(8,128)} %get-tuple-element.32), channel_id=1, source_target_pairs={{1,0},{2,1},{3,2},{4,3},{5,4},{6,5},{7,6},{8,7},{9,8},{10,9},{11,1... | collective-permute-start | bytes 12296 | tf_op jit(solution)/shard_map/ppermute | solution.py:20
  43.2 4.6 collective-permute-start.3
  49.8 258.0 %all-reduce.3.cloned.1.call-start = ((), (), s32[]{:S(2)}) async-start(), calls=%async_computation.1 | async-start | bytes 131072 | tf_op jit(solution)/shard_map/psum | solution.py:135
  120.1 398.5 %all-reduce.5.cloned.1.call-start = ((), (), s32[]{:S(2)}) async-start(), calls=%async_computation.2 | async-start | bytes 131072 | tf_op jit(solution)/shard_map/psum | solution.py:135
Sparse Core Ops, SparseCore 0:
  49.9 65.4 all-gather.1
  120.2 187.4 all-reduce.2
  338.5 180.0 all-reduce.4

commit v2 on v1

--- a/solution.py
+++ b/solution.py
@@ -1,3 +1,4 @@
+import functools
 import math
 
 import jax
@@ -10,6 +11,7 @@
 HALO = 128
 LANES = 128
 WIDE = 256
+CORES = 2
 
 highest = lax.Precision.HIGHEST
 
@@ -131,30 +133,237 @@
     )(low, probes, high, connectivity, sensitivity, obs_weight, prior_weight.reshape(1, -1))
 
 
-def gram_over_space(partial_value):
-    return lax.psum(partial_value, "space")
-
-
-def orthonormal(rows, reduce_gram):
-    gram_first = reduce_gram(
-        jnp.dot(rows, rows.T, precision=highest, preferred_element_type=jnp.float32)
-    )
-    lower_first = jnp.linalg.cholesky(gram_first)
-    basis_first = lax.linalg.triangular_solve(lower_first, rows, left_side=True, lower=True)
-    gram_second = reduce_gram(
-        jnp.dot(basis_first, basis_first.T, precision=highest, preferred_element_type=jnp.float32)
-    )
-    lower_second = jnp.linalg.cholesky(gram_second)
-    basis = lax.linalg.triangular_solve(lower_second, basis_first, left_side=True, lower=True)
-    factor = jnp.dot(
-        lower_first, lower_second, precision=highest, preferred_element_type=jnp.float32
-    ).T
-    return (basis, factor)
+SUBLANES = 8
+SLICE = 2.0**-8
+PROBE_SLICES = 4
+GRAM_SLICES = 5
+INVERSE_SLICES = 4
+FIRST_SLICES = 5
+
+
+def power_of_two(value):
+    return jnp.exp(value * math.log(2.0)).astype(jnp.bfloat16).astype(jnp.float32)
+
+
+def bound_of(magnitude):
+    return power_of_two(jnp.floor(jnp.log(magnitude) * (1.0 / math.log(2.0))) + 1.0)
+
+
+def sliced(value, bound, count, late=None, late_at=0):
+    sigma = bound * (1.5 * 2.0**16)
+    slices = []
+    for k in range(count):
+        if late is not None and k == late_at:
+            value = value + late
+        piece = (value + sigma) - sigma
+        slices.append(piece)
+        value = value - piece
+        sigma = sigma * SLICE
+    return slices
+
+
+def two_sum(a, b):
+    total = a + b
+    part = total - a
+    return total, (a - (total - part)) + (b - part)
+
+
+def added(left, right):
+    total, error = two_sum(left[0], right[0])
+    error = error + (left[1] + right[1])
+    high = total + error
+    return high, error - (high - total)
+
+
+def add_levels(blocks, rows, columns, levels):
+    high = low = None
+    for level in range(levels):
+        part = None
+        for a in range(rows):
+            b = level - a
+            if 0 <= b < columns:
+                part = blocks(a, b) if part is None else part + blocks(a, b)
+        if high is None:
+            high, low = part, jnp.zeros_like(part)
+        else:
+            high, error = two_sum(high, part)
+            low = low + error
+    total = high + low
+    return total, low - (total - high)
+
+
+def block_reader(products, size):
+    return lambda a, b: products[a * size : (a + 1) * size, b * size : (b + 1) * size]
+
+
+def gram_kernel(rows_ref, pair_ref):
+    rows = rows_ref[...]
+    size = rows.shape[0]
+    bound = bound_of(jnp.max(jnp.abs(rows), axis=1, keepdims=True))
+    stacked = jnp.concatenate(sliced(rows, bound, PROBE_SLICES), axis=0).astype(jnp.bfloat16)
+    products = lax.dot_general(
+        stacked, stacked, (((1,), (1,)), ((), ())), preferred_element_type=jnp.float32
+    )
+    high, low = add_levels(block_reader(products, size), PROBE_SLICES, PROBE_SLICES, 5)
+    parts, double, _ = pair_ref.shape
+    count = double // 2
+    for part in range(parts):
+        pair_ref[part, :count, :] = high[part * count : (part + 1) * count, :]
+        pair_ref[part, count:, :] = low[part * count : (part + 1) * count, :]
+
+
+def pairs_added(pairs):
+    while len(pairs) > 1:
+        joined = [added(a, b) for a, b in zip(pairs[::2], pairs[1::2])]
+        pairs = joined + pairs[len(pairs) // 2 * 2 :]
+    return pairs[0]
+
+
+def halves(block):
+    count = block.shape[0] // 2
+    return block[:count, :], block[count:, :]
+
+
+def sum_kernel(parts_ref, total_ref):
+    high, low = pairs_added([halves(parts_ref[k]) for k in range(parts_ref.shape[0])])
+    total_ref[...] = jnp.concatenate([high, low], axis=0)
+
+
+def spread_kernel(own_ref, other_ref, copies_ref):
+    high, low = added(halves(own_ref[...]), halves(other_ref[...]))
+    total = jnp.concatenate([high, low], axis=0)
+    for k in range(copies_ref.shape[0]):
+        copies_ref[k] = total
+
+
+def sum_spread_kernel(parts_ref, copies_ref):
+    high, low = pairs_added([halves(parts_ref[k]) for k in range(parts_ref.shape[0])])
+    total = jnp.concatenate([high, low], axis=0)
+    for k in range(copies_ref.shape[0]):
+        copies_ref[k] = total
+
+
+def triangles(gram):
+    size = gram.shape[0]
+    tiles = [gram[k * SUBLANES : (k + 1) * SUBLANES, :] for k in range(size // SUBLANES)]
+    pivots = [jnp.ones((SUBLANES, size), jnp.float32) for _ in tiles]
+    lane = lax.broadcasted_iota(jnp.int32, (SUBLANES, size), 1)
+    sub = lax.broadcasted_iota(jnp.int32, (SUBLANES, size), 0)
+    for j in range(size):
+        own, at = divmod(j, SUBLANES)
+        here = lane == j
+        row = jnp.broadcast_to(tiles[own][at : at + 1, :], (SUBLANES, size))
+        pivot = jnp.broadcast_to(row[:, j : j + 1], (SUBLANES, size))
+        scaled = jnp.where(here, 1.0, row) * (1.0 / pivot)
+        for k in range(own, len(tiles)):
+            column = jnp.broadcast_to(tiles[k][:, j : j + 1], (SUBLANES, size))
+            clear = here
+            if k == own:
+                column = jnp.where(sub > at, column, 0.0)
+                clear = here & (sub > at)
+                pivots[k] = jnp.where(sub == at, pivot, pivots[k])
+            tiles[k] = jnp.where(clear, 0.0, tiles[k]) - column * scaled
+    upper, inverse = [], []
+    for k, tile in enumerate(tiles):
+        root = lax.rsqrt(pivots[k])
+        root = root * (1.5 - 0.5 * pivots[k] * root * root)
+        row = sub + k * SUBLANES
+        upper.append(jnp.where(lane >= row, tile * root, 0.0))
+        inverse.append(jnp.where(lane > row, 0.0, jnp.where(lane == row, root, tile * root)))
+    return jnp.concatenate(upper, axis=0), jnp.concatenate(inverse, axis=0)
+
+
+def exact(a, b):
+    return jnp.dot(a, b, precision=highest, preferred_element_type=jnp.float32)
+
+
+def basis_kernel(scale, pair_ref, rows_ref, basis_ref, factor_ref):
+    parts, double, size = pair_ref.shape
+    count = double // 2
+    high = jnp.concatenate([pair_ref[k, :count, :] for k in range(parts)], axis=0)
+    low = jnp.concatenate([pair_ref[k, count:, :] for k in range(parts)], axis=0)
+    lane = lax.broadcasted_iota(jnp.int32, (size, size), 1)
+    sub = lax.broadcasted_iota(jnp.int32, (size, size), 0)
+    diagonal = jnp.where(lane == sub, high, 0.0)
+    down = jnp.floor(jnp.log(jnp.max(diagonal, axis=1, keepdims=True)) * (0.5 / math.log(2.0)))
+    across = jnp.floor(jnp.log(jnp.max(diagonal, axis=0, keepdims=True)) * (0.5 / math.log(2.0)))
+    shrink = power_of_two(-down)
+    shrink_across = power_of_two(-across)
+    four = jnp.where(shrink > 0.0, 4.0, 8.0)
+    high = high * shrink * shrink_across
+    low = low * shrink * shrink_across
+
+    upper_first, inverse_first = triangles(high)
+
+    gram_slices = sliced(high, four, GRAM_SLICES, late=low, late_at=3)
+    bound = bound_of(jnp.max(jnp.abs(inverse_first), axis=1, keepdims=True))
+    inverse_slices = sliced(inverse_first, bound, INVERSE_SLICES)
+    gram_stack = jnp.concatenate(gram_slices, axis=0).astype(jnp.bfloat16)
+    inverse_stack = jnp.concatenate(inverse_slices, axis=0).astype(jnp.bfloat16)
+    products = lax.dot_general(
+        gram_stack, inverse_stack, (((1,), (1,)), ((), ())), preferred_element_type=jnp.float32
+    )
+    lower_high, lower_low = add_levels(
+        block_reader(products, size), GRAM_SLICES, INVERSE_SLICES, 6
+    )
+    lower_slices = sliced(lower_high, four, FIRST_SLICES, late=lower_low, late_at=3)
+    lower_stack = jnp.concatenate(lower_slices, axis=1).astype(jnp.bfloat16)
+    products = jnp.dot(inverse_stack, lower_stack, preferred_element_type=jnp.float32)
+    gram_second, rest = add_levels(
+        block_reader(products, size), INVERSE_SLICES, FIRST_SLICES, 5
+    )
+    gram_second = gram_second + rest
+
+    upper_second, inverse_second = triangles(gram_second)
+    basis_first = exact(inverse_first, rows_ref[...] * shrink)
+    basis = exact(inverse_second, basis_first)
+    basis_ref[...] = basis * scale
+    factor = exact(upper_second, upper_first)
+    factor_ref[...] = factor * (power_of_two(across) * (1.0 / scale))
+
+
+def in_vmem(kernel, name, out_shape, *operands):
+    vmem = pl.BlockSpec(memory_space=pltpu.VMEM)
+    single = not isinstance(out_shape, tuple)
+    return pl.pallas_call(
+        kernel,
+        out_shape=out_shape,
+        in_specs=[vmem] * len(operands),
+        out_specs=vmem if single else tuple(vmem for _ in out_shape),
+        name=name,
+    )(*operands)
+
+
+def orthonormal(rows, scale):
+    size = rows.shape[0]
+    parts = lax.axis_size("probe")
+    count = 2 * size // parts
+    places = lax.axis_size("space")
+    pair = jax.ShapeDtypeStruct((parts, count, size), jnp.float32)
+    one = jax.ShapeDtypeStruct((count, size), jnp.float32)
+    levels = places // CORES
+    copies = jax.ShapeDtypeStruct((levels, count, size), jnp.float32)
+    gram = in_vmem(gram_kernel, "gram", pair, rows)
+    gram = lax.all_to_all(gram, "probe", 0, 0, tiled=True)
+    own = in_vmem(sum_kernel, "probe_sum", one, gram)
+    other = lax.ppermute(own, "space", [(k, k ^ 1) for k in range(places)])
+    spread = in_vmem(spread_kernel, "core_sum", copies, own, other)
+    groups = [[core + CORES * k for k in range(levels)] for core in range(CORES)]
+    spread = lax.all_to_all(spread, "space", 0, 0, tiled=True, axis_index_groups=groups)
+    whole = in_vmem(sum_spread_kernel, "space_sum", pair, spread)
+    whole = lax.all_to_all(whole, "probe", 0, 0, tiled=True)
+    return in_vmem(
+        functools.partial(basis_kernel, scale), "basis",
+        (
+            jax.ShapeDtypeStruct(rows.shape, jnp.float32),
+            jax.ShapeDtypeStruct((size, size), jnp.float32),
+        ),
+        whole, rows,
+    )
 
 
 def on_device(probes, sensitivity, obs_weight, prior_weight, connectivity):
     node_count = probes.shape[1]
-    probe_count = probes.shape[0]
     low = shifted(probes[:, node_count - HALO :], "space", 1)
     high = shifted(probes[:, :HALO], "space", -1)
     images, lower, upper = element_images(
@@ -165,10 +374,9 @@
     images = images.at[:, node_count - HALO :].add(lower_rim)
     images = images.at[:, :HALO].add(upper_rim)
     scale = math.sqrt(float(node_count * lax.axis_size("space")))
-    whole = lax.all_gather(images, "probe", axis=0, tiled=True)
-    basis, factor = orthonormal(whole, gram_over_space)
-    basis = lax.dynamic_slice_in_dim(basis, lax.axis_index("probe") * probe_count, probe_count, 0)
-    return (basis * scale, factor / scale)
+    rows = lax.all_to_all(images, "probe", 1, 0, tiled=True)
+    basis, factor = orthonormal(rows, scale)
+    return lax.all_to_all(basis, "probe", 0, 1, tiled=True), factor
 
 
 def solution(mesh):

time: 556 us -> 171 us (0.31)
  the two profiles are of different devices: /device:TPU:1 before, /device:TPU:32 now
where the time goes in v2:
time: 171 us; the launch traced here: 170 us
  blocking collectives  78.7 us (46%)
  Pallas kernels  64.6 us (38%)
  starting transfers between devices  10.7 us (6%)
  waiting for transfers between devices  8.88 us (5%)
  other arithmetic  3.85 us (2%)
  local copies, waits for them, and re-layouts  2.56 us (1%)
    pallas_call x5, Pallas kernels, in_vmem(): pl.pallas_call(kernel, out_shape=out_shape, in_specs=[vmem] * len(operand...  43.6 us
    all_to_all x1, blocking collectives, orthonormal(): lax.all_to_all(spread, 'space', 0, 0, tiled=True, axis_index_groups=groups)  30.8 us
    pallas_call x1, Pallas kernels, element_images(): pl.pallas_call(element_kernel, out_shape=(jax.ShapeDtypeStruct(probes.sha...  21 us
    all_to_all x1, blocking collectives, orthonormal(): gram = lax.all_to_all(gram, 'probe', 0, 0, tiled=True)  12.2 us
    all_to_all x1, blocking collectives, orthonormal(): whole = lax.all_to_all(whole, 'probe', 0, 0, tiled=True)  12.2 us
    all_to_all x1, blocking collectives, on_device(): rows = lax.all_to_all(images, 'probe', 1, 0, tiled=True)  12.2 us
    all_to_all x1, blocking collectives, on_device(): return (lax.all_to_all(basis, 'probe', 0, 1, tiled=True), factor)  11.5 us
    ppermute x4, starting transfers between devices, shifted(): return lax.ppermute(block, axis, route)  8.75 us
  transfers between devices with their start and end apart: 5, of which 3 were waited for; matrix products, arithmetic and copies ran while one was open for 1% of the time, Pallas kernels for 0%

profile of v2, /device:TPU:32, one launch (start us, length us, event | category | flops | bytes accessed | tf_op | source)
XLA Modules:
  0.0 170.0 jit_solution(15528322753263988872)
XLA Ops:
  0.6 0.7 fusion.1
  1.3 1.9 %collective-permute-start.1 = (f32[8,128]{1,0:T(8,128)S(1)}, f32[8,128]{1,0:T(8,128)S(1)}, u32[]{:S(2)}, u32[]{:S(2)}) collective-permute-start(f32[8,128]{1,0:T(8,128)S(1)} %get-tuple-element.36), channel_id=1, source_target_pairs={{1,0},{2,1},{3,2},{4,3},{5,4},{6,5},{7,6},{8,7},{9,8},{10,9},{11,1... | collective-permute-start | bytes 12296 | tf_op jit(solution)/shard_map/ppermute | solution.py:22
  3.3 2.4 %collective-permute-start = (f32[8,128]{1,0:T(8,128)S(1)}, f32[8,128]{1,0:T(8,128)S(1)}, u32[]{:S(2)}, u32[]{:S(2)}) collective-permute-start(f32[8,128]{1,0:T(8,128)S(1)} %get-tuple-element.37), channel_id=1, source_target_pairs={{0,1},{1,2},{2,3},{3,4},{4,5},{5,6},{6,7},{7,8},{8,9},{9,10},{10,1... | collective-permute-start | bytes 12296 | tf_op jit(solution)/shard_map/ppermute | solution.py:22
  5.7 0.0 collective-permute-done.1.high_ref
  5.7 0.0 copy-start.1
  5.7 6.3 %collective-permute-done.low_ref = f32[8,128]{1,0:T(8,128)S(1)} collective-permute-done((f32[8,128]{1,0:T(8,128)S(1)}, f32[8,128]{1,0:T(8,128)S(1)}, u32[]{:S(2)}, u32[]{:S(2)}) %collective-permute-start) | collective-permute-done | bytes 4128 | tf_op jit(solution)/shard_map/ppermute | solution.py:22
  12.0 0.0 copy-start.2
  12.0 0.0 copy-done.1
  12.0 0.6 copy-done.2
  12.6 21.0 %element_images.1 = (f32[8,4096]{1,0:T(8,128)}, f32[8,128]{1,0:T(8,128)}, f32[8,128]{1,0:T(8,128)}) custom-call(f32[8,128]{1,0:T(8,128)} %copy-done.2, f32[8,4096]{1,0:T(8,128)} %probes_ref.1, f32[8,128]{1,0:T(8,128)} %copy-done.1, s32[8,2048]{1,0:T(8,128)} %connectivity_ref.1, f32[8,8,2048]{2,1,0:T(8,128)} %sensitivity_ref.1, f32[8,2048]{1,0:T(8,128)} %weight_ref.1, ...), custom_call_target="tpu_custom_call" | custom-call | tf_op jit(solution)/shard_map/element_images/pallas_call | solution.py:122
  33.6 0.0 copy-start.3
  33.6 2.0 %collective-permute-start.2 = (f32[8,128]{1,0:T(8,128)}, f32[8,128]{1,0:T(8,128)S(1)}, u32[]{:S(2)}, u32[]{:S(2)}) collective-permute-start(f32[8,128]{1,0:T(8,128)} %get-tuple-element.32), channel_id=1, source_target_pairs={{1,0},{2,1},{3,2},{4,3},{5,4},{6,5},{7,6},{8,7},{9,8},{10,9},{11,1... | collective-permute-start | bytes 12296 | tf_op jit(solution)/shard_map/ppermute | solution.py:22
  35.6 0.6 compare_reduce_fusion
  36.2 0.0 copy-done.3
  36.2 2.4 %collective-permute-start.3 = (f32[8,128]{1,0:T(8,128)S(1)}, f32[8,128]{1,0:T(8,128)S(1)}, u32[]{:S(2)}, u32[]{:S(2)}) collective-permute-start(f32[8,128]{1,0:T(8,128)S(1)} %copy-done.3), channel_id=1, source_target_pairs={{0,1},{1,2},{2,3},{3,4},{4,5},{5,6},{6,7},{7,8},{8,9},{9,10},{10,1... | collective-permute-start | bytes 12296 | tf_op jit(solution)/shard_map/ppermute | solution.py:22
  38.7 0.0 collective-permute-done.2
  38.7 1.3 add_dynamic-update-slice_fusion
  39.9 1.2 collective-permute-done.3
  41.2 1.9 %fusion = f32[8,4096]{1,0:T(8,128)} fusion(f32[8,4096]{1,0:T(8,128)} %add_dynamic-update-slice_fusion, f32[8,128]{1,0:T(8,128)S(1)} %collective-permute-done.3, pred[]{:T(512)} %compare_reduce_fusion), kind=kLoop, calls=%fused_computation.1 | loop fusion | flops 2048 | bytes 12800 | tf_op jit(solution)/shard_map/scatter-add | solution.py:375
  43.1 12.2 %all_to_all.53 = f32[8,16,256]{2,0,1:T(8,128)} all-to-all(f32[8,16,256]{2,0,1:T(8,128)} %bitcast.12), channel_id=1, replica_groups=mesh['probe'=16,'space'=32] {'probe'}, dimensions={1} | all-to-all | bytes 262144 | tf_op jit(solution)/shard_map/all_to_all | solution.py:377
  55.2 2.0 %gram.1 = f32[16,16,128]{2,1,0:T(8,128)} custom-call(f32[128,256]{1,0:T(8,128)} %bitcast.9), custom_call_target="tpu_custom_call" | custom-call | tf_op jit(solution)/shard_map/gram/pallas_call | solution.py:328
  57.3 12.2 %all_to_all.54.parts_ref = f32[16,16,128]{2,1,0:T(8,128)} all-to-all(f32[16,16,128]{2,1,0:T(8,128)} %gram.1), channel_id=1, replica_groups=mesh['probe'=16,'space'=32] {'probe'}, dimensions={0} | all-to-all | bytes 262144 | tf_op jit(solution)/shard_map/all_to_all | solution.py:347
  69.4 1.5 probe_sum.1.own_ref
  71.0 1.9 %collective-permute-start.4 = (f32[16,128]{1,0:T(8,128)}, f32[16,128]{1,0:T(8,128)S(1)}, u32[]{:S(2)}, u32[]{:S(2)}) collective-permute-start(f32[16,128]{1,0:T(8,128)} %probe_sum.1.own_ref), channel_id=1, source_target_pairs={{0,1},{1,0},{2,3},{3,2},{4,5},{5,4},{6,7},{7,6},{8,9},{9,8},{10,11... | collective-permute-start | bytes 24584 | tf_op jit(solution)/shard_map/ppermute | solution.py:349
  72.9 1.3 collective-permute-done.4.other_ref
  74.2 0.0 copy-start
  74.2 0.6 copy-done
  74.8 1.4 core_sum.1
  76.2 30.8 %all_to_all.55.parts_ref = f32[16,16,128]{2,1,0:T(8,128)} all-to-all(f32[16,16,128]{2,1,0:T(8,128)} %core_sum.1), channel_id=1, replica_groups={{0,2,4,6,8,10,12,14,16,18,20,22,24,26,28,30},{1,3,5,7,9,11,13,15,17,19,..., dimensions={0} | all-to-all | bytes 262144 | tf_op jit(solution)/shard_map/all_to_all | solution.py:352
  107.0 1.6 space_sum.1
  108.6 12.2 %all_to_all.56.pair_ref = f32[16,16,128]{2,1,0:T(8,128)} all-to-all(f32[16,16,128]{2,1,0:T(8,128)} %space_sum.1), channel_id=1, replica_groups=mesh['probe'=16,'space'=32] {'probe'}, dimensions={0} | all-to-all | bytes 262144 | tf_op jit(solution)/shard_map/all_to_all | solution.py:354
  120.8 37.1 %basis.1 = (f32[128,256]{1,0:T(8,128)}, f32[128,128]{1,0:T(8,128)}) custom-call(f32[16,16,128]{2,1,0:T(8,128)} %all_to_all.56.pair_ref, f32[128,256]{1,0:T(8,128)} %bitcast.10), custom_call_target="tpu_custom_call" | custom-call | tf_op jit(solution)/shard_map/basis/pallas_call | solution.py:328
  157.8 11.5 %all_to_all.57 = f32[16,8,256]{2,1,0:T(8,128)S(1)} all-to-all(f32[16,8,256]{2,1,0:T(8,128)} %bitcast.13), channel_id=1, replica_groups=mesh['probe'=16,'space'=32] {'probe'}, dimensions={0} | all-to-all | bytes 262144 | tf_op jit(solution)/shard_map/all_to_all | solution.py:379
  169.3 0.7 copy.10
Async XLA Ops:
  1.3 4.3 %collective-permute-start.1 = (f32[8,128]{1,0:T(8,128)S(1)}, f32[8,128]{1,0:T(8,128)S(1)}, u32[]{:S(2)}, u32[]{:S(2)}) collective-permute-start(f32[8,128]{1,0:T(8,128)S(1)} %get-tuple-element.36), channel_id=1, source_target_pairs={{1,0},{2,1},{3,2},{4,3},{5,4},{6,5},{7,6},{8,7},{9,8},{10,9},{11,1... | collective-permute-start | bytes 12296 | tf_op jit(solution)/shard_map/ppermute | solution.py:22
  3.3 8.7 %collective-permute-start = (f32[8,128]{1,0:T(8,128)S(1)}, f32[8,128]{1,0:T(8,128)S(1)}, u32[]{:S(2)}, u32[]{:S(2)}) collective-permute-start(f32[8,128]{1,0:T(8,128)S(1)} %get-tuple-element.37), channel_id=1, source_target_pairs={{0,1},{1,2},{2,3},{3,4},{4,5},{5,6},{6,7},{7,8},{8,9},{9,10},{10,1... | collective-permute-start | bytes 12296 | tf_op jit(solution)/shard_map/ppermute | solution.py:22
  5.7 6.3 %copy-start.1 = (f32[8,128]{1,0:T(8,128)}, f32[8,128]{1,0:T(8,128)S(1)}, u32[]{:S(2)}) copy-start(f32[8,128]{1,0:T(8,128)S(1)} %collective-permute-done.1.high_ref) | copy-start | bytes 12292
  12.0 0.6 copy-start.2
  33.6 2.7 %copy-start.3 = (f32[8,128]{1,0:T(8,128)S(1)}, f32[8,128]{1,0:T(8,128)}, u32[]{:S(2)}) copy-start(f32[8,128]{1,0:T(8,128)} %get-tuple-element.33) | copy-start | bytes 12292
  33.6 5.1 %collective-permute-start.2 = (f32[8,128]{1,0:T(8,128)}, f32[8,128]{1,0:T(8,128)S(1)}, u32[]{:S(2)}, u32[]{:S(2)}) collective-permute-start(f32[8,128]{1,0:T(8,128)} %get-tuple-element.32), channel_id=1, source_target_pairs={{1,0},{2,1},{3,2},{4,3},{5,4},{6,5},{7,6},{8,7},{9,8},{10,9},{11,1... | collective-permute-start | bytes 12296 | tf_op jit(solution)/shard_map/ppermute | solution.py:22
  36.2 4.9 %collective-permute-start.3 = (f32[8,128]{1,0:T(8,128)S(1)}, f32[8,128]{1,0:T(8,128)S(1)}, u32[]{:S(2)}, u32[]{:S(2)}) collective-permute-start(f32[8,128]{1,0:T(8,128)S(1)} %copy-done.3), channel_id=1, source_target_pairs={{0,1},{1,2},{2,3},{3,4},{4,5},{5,6},{6,7},{7,8},{8,9},{9,10},{10,1... | collective-permute-start | bytes 12296 | tf_op jit(solution)/shard_map/ppermute | solution.py:22
  71.0 3.3 %collective-permute-start.4 = (f32[16,128]{1,0:T(8,128)}, f32[16,128]{1,0:T(8,128)S(1)}, u32[]{:S(2)}, u32[]{:S(2)}) collective-permute-start(f32[16,128]{1,0:T(8,128)} %probe_sum.1.own_ref), channel_id=1, source_target_pairs={{0,1},{1,0},{2,3},{3,2},{4,5},{5,4},{6,7},{7,6},{8,9},{9,8},{10,11... | collective-permute-start | bytes 24584 | tf_op jit(solution)/shard_map/ppermute | solution.py:349
  74.2 0.6 copy-start

commit v3 on v2

--- a/solution.py
+++ b/solution.py
@@ -134,6 +134,7 @@
 
 
 SUBLANES = 8
+GROUP = 2
 SLICE = 2.0**-8
 PROBE_SLICES = 4
 GRAM_SLICES = 5
@@ -243,41 +244,87 @@
         copies_ref[k] = total
 
 
-def triangles(gram):
+def eliminate_group(tiles, pivots, at):
+    shape = tiles[0].shape
+    lane = lax.broadcasted_iota(jnp.int32, shape, 1)
+    sub = lax.broadcasted_iota(jnp.int32, shape, 0)
+    chosen = range(GROUP)
+    columns = [[jnp.broadcast_to(tile[:, at + r : at + r + 1], shape) for r in chosen] for tile in tiles]
+    entry = [
+        [jnp.broadcast_to(columns[0][c][at + r : at + r + 1, :], shape) for c in chosen] for r in chosen
+    ]
+    rows = [jnp.broadcast_to(tiles[0][at + r : at + r + 1, :], shape) for r in chosen]
+    factor = [[None] * GROUP for _ in chosen]
+    scaled = []
+    for s in chosen:
+        over = 1.0 / entry[s][s]
+        here = lane == at + s
+        with_one = jnp.where(here, 1.0, rows[s])
+        for r in range(s + 1, GROUP):
+            factor[s][r] = entry[s][r] * over
+            for c in range(r, GROUP):
+                entry[r][c] = entry[r][c] - factor[s][r] * entry[s][c]
+            rows[r] = jnp.where(here, 0.0, rows[r]) - factor[s][r] * with_one
+        later = (lane > at + s) & (lane < at + GROUP)
+        scaled.append(jnp.where(later, 0.0, with_one) * over)
+    inside = (lane >= at) & (lane < at + GROUP)
+    done = []
+    for k, tile in enumerate(tiles):
+        clear = inside
+        if k == 0:
+            below = sub >= at + GROUP
+            clear = inside & below
+        new = jnp.where(clear, 0.0, tile)
+        own = list(columns[k])
+        for s in chosen:
+            for r in range(s + 1, GROUP):
+                own[r] = own[r] - own[s] * factor[s][r]
+        for s in chosen:
+            value = jnp.where(below, own[s], 0.0) if k == 0 else own[s]
+            new = new - value * scaled[s]
+        if k == 0:
+            for s in chosen:
+                new = jnp.where(sub == at + s, rows[s], new)
+                pivots = jnp.where(sub == at + s, entry[s][s], pivots)
+        done.append(new)
+    return done, pivots
+
+
+def triangles(gram, tile_ref, pivot_ref):
     size = gram.shape[0]
-    tiles = [gram[k * SUBLANES : (k + 1) * SUBLANES, :] for k in range(size // SUBLANES)]
-    pivots = [jnp.ones((SUBLANES, size), jnp.float32) for _ in tiles]
-    lane = lax.broadcasted_iota(jnp.int32, (SUBLANES, size), 1)
-    sub = lax.broadcasted_iota(jnp.int32, (SUBLANES, size), 0)
-    for j in range(size):
-        own, at = divmod(j, SUBLANES)
-        here = lane == j
-        row = jnp.broadcast_to(tiles[own][at : at + 1, :], (SUBLANES, size))
-        pivot = jnp.broadcast_to(row[:, j : j + 1], (SUBLANES, size))
-        scaled = jnp.where(here, 1.0, row) * (1.0 / pivot)
-        for k in range(own, len(tiles)):
-            column = jnp.broadcast_to(tiles[k][:, j : j + 1], (SUBLANES, size))
-            clear = here
-            if k == own:
-                column = jnp.where(sub > at, column, 0.0)
-                clear = here & (sub > at)
-                pivots[k] = jnp.where(sub == at, pivot, pivots[k])
-            tiles[k] = jnp.where(clear, 0.0, tiles[k]) - column * scaled
-    upper, inverse = [], []
-    for k, tile in enumerate(tiles):
-        root = lax.rsqrt(pivots[k])
-        root = root * (1.5 - 0.5 * pivots[k] * root * root)
-        row = sub + k * SUBLANES
-        upper.append(jnp.where(lane >= row, tile * root, 0.0))
-        inverse.append(jnp.where(lane > row, 0.0, jnp.where(lane == row, root, tile * root)))
-    return jnp.concatenate(upper, axis=0), jnp.concatenate(inverse, axis=0)
+    count = size // SUBLANES
+    tiles = [gram[k * SUBLANES : (k + 1) * SUBLANES, :] for k in range(count)]
+
+    def block(step, tiles):
+        tiles = list(tiles)
+        pivots = jnp.ones((SUBLANES, size), jnp.float32)
+        for at in range(0, SUBLANES, GROUP):
+            tiles, pivots = eliminate_group(tiles, pivots, at)
+        place = pl.ds(pl.multiple_of(step * SUBLANES, SUBLANES), SUBLANES)
+        tile_ref[place, :] = pltpu.roll(tiles[0], step * SUBLANES, 1)
+        pivot_ref[place, :] = pivots
+        tiles = [pltpu.roll(tile, size - SUBLANES, 1) for tile in tiles]
+        return tuple(tiles[1:] + tiles[:1])
+
+    half = count // 2
+    tiles = lax.fori_loop(0, half, block, tuple(tiles))
+    lax.fori_loop(half, count, block, tuple(tiles[:half]))
+    tile, pivot = tile_ref[...], pivot_ref[...]
+    lane = lax.broadcasted_iota(jnp.int32, tile.shape, 1)
+    row = lax.broadcasted_iota(jnp.int32, tile.shape, 0)
+    root = lax.rsqrt(pivot)
+    root = root * (1.5 - 0.5 * pivot * root * root)
+    scaled = tile * root
+    upper = jnp.where(lane > row, scaled, jnp.where(lane == row, pivot * root, 0.0))
+    inverse = jnp.where(lane < row, scaled, jnp.where(lane == row, root, 0.0))
+    return upper, inverse
 
 
 def exact(a, b):
     return jnp.dot(a, b, precision=highest, preferred_element_type=jnp.float32)
 
 
-def basis_kernel(scale, pair_ref, rows_ref, basis_ref, factor_ref):
+def basis_kernel(scale, pair_ref, rows_ref, basis_ref, factor_ref, tile_ref, pivot_ref):
     parts, double, size = pair_ref.shape
     count = double // 2
     high = jnp.concatenate([pair_ref[k, :count, :] for k in range(parts)], axis=0)
@@ -293,7 +340,7 @@
     high = high * shrink * shrink_across
     low = low * shrink * shrink_across
 
-    upper_first, inverse_first = triangles(high)
+    upper_first, inverse_first = triangles(high, tile_ref, pivot_ref)
 
     gram_slices = sliced(high, four, GRAM_SLICES, late=low, late_at=3)
     bound = bound_of(jnp.max(jnp.abs(inverse_first), axis=1, keepdims=True))
@@ -314,7 +361,7 @@
     )
     gram_second = gram_second + rest
 
-    upper_second, inverse_second = triangles(gram_second)
+    upper_second, inverse_second = triangles(gram_second, tile_ref, pivot_ref)
     basis_first = exact(inverse_first, rows_ref[...] * shrink)
     basis = exact(inverse_second, basis_first)
     basis_ref[...] = basis * scale
@@ -322,7 +369,7 @@
     factor_ref[...] = factor * (power_of_two(across) * (1.0 / scale))
 
 
-def in_vmem(kernel, name, out_shape, *operands):
+def in_vmem(kernel, name, out_shape, *operands, scratch=()):
     vmem = pl.BlockSpec(memory_space=pltpu.VMEM)
     single = not isinstance(out_shape, tuple)
     return pl.pallas_call(
@@ -330,6 +377,7 @@
         out_shape=out_shape,
         in_specs=[vmem] * len(operands),
         out_specs=vmem if single else tuple(vmem for _ in out_shape),
+        scratch_shapes=scratch,
         name=name,
     )(*operands)
 
@@ -359,6 +407,7 @@
             jax.ShapeDtypeStruct((size, size), jnp.float32),
         ),
         whole, rows,
+        scratch=(pltpu.VMEM((size, size), jnp.float32),) * 2,
     )
 
 

time: 171 us -> 157 us (0.918)
  Pallas kernels: 64.6 us -> 50.4 us
    pallas_call x5, Pallas kernels: 43.6 us -> 29.4 us  [in_vmem(): pl.pallas_call(kernel, out_shape=out_shape, in_specs=[vmem] * len(operand...]
where the time goes in v3:
time: 157 us; the launch traced here: 156 us
  blocking collectives  78.7 us (50%)
  Pallas kernels  50.4 us (32%)
  starting transfers between devices  10.7 us (7%)
  waiting for transfers between devices  8.88 us (6%)
  other arithmetic  3.85 us (2%)
  local copies, waits for them, and re-layouts  2.56 us (2%)
    all_to_all x1, blocking collectives, orthonormal(): lax.all_to_all(spread, 'space', 0, 0, tiled=True, axis_index_groups=groups)  30.8 us
    pallas_call x5, Pallas kernels, in_vmem(): pl.pallas_call(kernel, out_shape=out_shape, in_specs=[vmem] * len(operand...  29.4 us
    pallas_call x1, Pallas kernels, element_images(): pl.pallas_call(element_kernel, out_shape=(jax.ShapeDtypeStruct(probes.sha...  21 us
    all_to_all x1, blocking collectives, orthonormal(): gram = lax.all_to_all(gram, 'probe', 0, 0, tiled=True)  12.2 us
    all_to_all x1, blocking collectives, orthonormal(): whole = lax.all_to_all(whole, 'probe', 0, 0, tiled=True)  12.2 us
    all_to_all x1, blocking collectives, on_device(): rows = lax.all_to_all(images, 'probe', 1, 0, tiled=True)  12.2 us
    all_to_all x1, blocking collectives, on_device(): return (lax.all_to_all(basis, 'probe', 0, 1, tiled=True), factor)  11.5 us
    ppermute x4, starting transfers between devices, shifted(): return lax.ppermute(block, axis, route)  8.75 us
  transfers between devices with their start and end apart: 5, of which 3 were waited for; matrix products, arithmetic and copies ran while one was open for 1% of the time, Pallas kernels for 0%

profile of v3, /device:TPU:32, one launch (start us, length us, event | category | flops | bytes accessed | tf_op | source)
XLA Modules:
  0.0 155.7 jit_solution(15707115183677656589)
XLA Ops:
  0.6 0.7 fusion.1
  1.3 1.9 %collective-permute-start.1 = (f32[8,128]{1,0:T(8,128)S(1)}, f32[8,128]{1,0:T(8,128)S(1)}, u32[]{:S(2)}, u32[]{:S(2)}) collective-permute-start(f32[8,128]{1,0:T(8,128)S(1)} %get-tuple-element.36), channel_id=1, source_target_pairs={{1,0},{2,1},{3,2},{4,3},{5,4},{6,5},{7,6},{8,7},{9,8},{10,9},{11,1... | collective-permute-start | bytes 12296 | tf_op jit(solution)/shard_map/ppermute | solution.py:22
  3.3 2.4 %collective-permute-start = (f32[8,128]{1,0:T(8,128)S(1)}, f32[8,128]{1,0:T(8,128)S(1)}, u32[]{:S(2)}, u32[]{:S(2)}) collective-permute-start(f32[8,128]{1,0:T(8,128)S(1)} %get-tuple-element.37), channel_id=1, source_target_pairs={{0,1},{1,2},{2,3},{3,4},{4,5},{5,6},{6,7},{7,8},{8,9},{9,10},{10,1... | collective-permute-start | bytes 12296 | tf_op jit(solution)/shard_map/ppermute | solution.py:22
  5.7 0.0 collective-permute-done.1.high_ref
  5.7 0.0 copy-start.1
  5.7 6.3 %collective-permute-done.low_ref = f32[8,128]{1,0:T(8,128)S(1)} collective-permute-done((f32[8,128]{1,0:T(8,128)S(1)}, f32[8,128]{1,0:T(8,128)S(1)}, u32[]{:S(2)}, u32[]{:S(2)}) %collective-permute-start) | collective-permute-done | bytes 4128 | tf_op jit(solution)/shard_map/ppermute | solution.py:22
  12.0 0.0 copy-start.2
  12.0 0.0 copy-done.1
  12.0 0.6 copy-done.2
  12.6 21.0 %element_images.1 = (f32[8,4096]{1,0:T(8,128)}, f32[8,128]{1,0:T(8,128)}, f32[8,128]{1,0:T(8,128)}) custom-call(f32[8,128]{1,0:T(8,128)} %copy-done.2, f32[8,4096]{1,0:T(8,128)} %probes_ref.1, f32[8,128]{1,0:T(8,128)} %copy-done.1, s32[8,2048]{1,0:T(8,128)} %connectivity_ref.1, f32[8,8,2048]{2,1,0:T(8,128)} %sensitivity_ref.1, f32[8,2048]{1,0:T(8,128)} %weight_ref.1, ...), custom_call_target="tpu_custom_call" | custom-call | tf_op jit(solution)/shard_map/element_images/pallas_call | solution.py:122
  33.6 0.0 copy-start.3
  33.6 2.0 %collective-permute-start.2 = (f32[8,128]{1,0:T(8,128)}, f32[8,128]{1,0:T(8,128)S(1)}, u32[]{:S(2)}, u32[]{:S(2)}) collective-permute-start(f32[8,128]{1,0:T(8,128)} %get-tuple-element.32), channel_id=1, source_target_pairs={{1,0},{2,1},{3,2},{4,3},{5,4},{6,5},{7,6},{8,7},{9,8},{10,9},{11,1... | collective-permute-start | bytes 12296 | tf_op jit(solution)/shard_map/ppermute | solution.py:22
  35.6 0.6 compare_reduce_fusion
  36.2 0.0 copy-done.3
  36.2 2.4 %collective-permute-start.3 = (f32[8,128]{1,0:T(8,128)S(1)}, f32[8,128]{1,0:T(8,128)S(1)}, u32[]{:S(2)}, u32[]{:S(2)}) collective-permute-start(f32[8,128]{1,0:T(8,128)S(1)} %copy-done.3), channel_id=1, source_target_pairs={{0,1},{1,2},{2,3},{3,4},{4,5},{5,6},{6,7},{7,8},{8,9},{9,10},{10,1... | collective-permute-start | bytes 12296 | tf_op jit(solution)/shard_map/ppermute | solution.py:22
  38.7 0.0 collective-permute-done.2
  38.7 1.3 add_dynamic-update-slice_fusion
  39.9 1.2 collective-permute-done.3
  41.2 1.9 %fusion = f32[8,4096]{1,0:T(8,128)} fusion(f32[8,4096]{1,0:T(8,128)} %add_dynamic-update-slice_fusion, f32[8,128]{1,0:T(8,128)S(1)} %collective-permute-done.3, pred[]{:T(512)} %compare_reduce_fusion), kind=kLoop, calls=%fused_computation.1 | loop fusion | flops 2048 | bytes 12800 | tf_op jit(solution)/shard_map/scatter-add | solution.py:424
  43.1 12.2 %all_to_all.53 = f32[8,16,256]{2,0,1:T(8,128)} all-to-all(f32[8,16,256]{2,0,1:T(8,128)} %bitcast.12), channel_id=1, replica_groups=mesh['probe'=16,'space'=32] {'probe'}, dimensions={1} | all-to-all | bytes 262144 | tf_op jit(solution)/shard_map/all_to_all | solution.py:426
  55.2 2.0 %gram.1 = f32[16,16,128]{2,1,0:T(8,128)} custom-call(f32[128,256]{1,0:T(8,128)} %bitcast.9), custom_call_target="tpu_custom_call" | custom-call | tf_op jit(solution)/shard_map/gram/pallas_call | solution.py:375
  57.3 12.2 %all_to_all.54.parts_ref = f32[16,16,128]{2,1,0:T(8,128)} all-to-all(f32[16,16,128]{2,1,0:T(8,128)} %gram.1), channel_id=1, replica_groups=mesh['probe'=16,'space'=32] {'probe'}, dimensions={0} | all-to-all | bytes 262144 | tf_op jit(solution)/shard_map/all_to_all | solution.py:395
  69.4 1.5 probe_sum.1.own_ref
  71.0 1.9 %collective-permute-start.4 = (f32[16,128]{1,0:T(8,128)}, f32[16,128]{1,0:T(8,128)S(1)}, u32[]{:S(2)}, u32[]{:S(2)}) collective-permute-start(f32[16,128]{1,0:T(8,128)} %probe_sum.1.own_ref), channel_id=1, source_target_pairs={{0,1},{1,0},{2,3},{3,2},{4,5},{5,4},{6,7},{7,6},{8,9},{9,8},{10,11... | collective-permute-start | bytes 24584 | tf_op jit(solution)/shard_map/ppermute | solution.py:397
  72.9 1.3 collective-permute-done.4.other_ref
  74.2 0.0 copy-start
  74.2 0.6 copy-done
  74.8 1.4 core_sum.1
  76.2 30.8 %all_to_all.55.parts_ref = f32[16,16,128]{2,1,0:T(8,128)} all-to-all(f32[16,16,128]{2,1,0:T(8,128)} %core_sum.1), channel_id=1, replica_groups={{0,2,4,6,8,10,12,14,16,18,20,22,24,26,28,30},{1,3,5,7,9,11,13,15,17,19,..., dimensions={0} | all-to-all | bytes 262144 | tf_op jit(solution)/shard_map/all_to_all | solution.py:400
  107.0 1.6 %space_sum.1 = f32[16,16,128]{2,1,0:T(8,128)} custom-call(f32[16,16,128]{2,1,0:T(8,128)} %all_to_all.55.parts_ref), custom_call_target="tpu_custom_call" | custom-call | tf_op jit(solution)/shard_map/space_sum/pallas_call | solution.py:375
  108.6 12.2 %all_to_all.56.pair_ref = f32[16,16,128]{2,1,0:T(8,128)} all-to-all(f32[16,16,128]{2,1,0:T(8,128)} %space_sum.1), channel_id=1, replica_groups=mesh['probe'=16,'space'=32] {'probe'}, dimensions={0} | all-to-all | bytes 262144 | tf_op jit(solution)/shard_map/all_to_all | solution.py:402
  120.8 22.9 %basis.1 = (f32[128,256]{1,0:T(8,128)}, f32[128,128]{1,0:T(8,128)}) custom-call(f32[16,16,128]{2,1,0:T(8,128)} %all_to_all.56.pair_ref, f32[128,256]{1,0:T(8,128)} %bitcast.10), custom_call_target="tpu_custom_call" | custom-call | tf_op jit(solution)/shard_map/basis/pallas_call | solution.py:375
  143.6 11.5 %all_to_all.57 = f32[16,8,256]{2,1,0:T(8,128)S(1)} all-to-all(f32[16,8,256]{2,1,0:T(8,128)} %bitcast.13), channel_id=1, replica_groups=mesh['probe'=16,'space'=32] {'probe'}, dimensions={0} | all-to-all | bytes 262144 | tf_op jit(solution)/shard_map/all_to_all | solution.py:428
  155.1 0.7 copy.10
Async XLA Ops:
  1.3 4.3 %collective-permute-start.1 = (f32[8,128]{1,0:T(8,128)S(1)}, f32[8,128]{1,0:T(8,128)S(1)}, u32[]{:S(2)}, u32[]{:S(2)}) collective-permute-start(f32[8,128]{1,0:T(8,128)S(1)} %get-tuple-element.36), channel_id=1, source_target_pairs={{1,0},{2,1},{3,2},{4,3},{5,4},{6,5},{7,6},{8,7},{9,8},{10,9},{11,1... | collective-permute-start | bytes 12296 | tf_op jit(solution)/shard_map/ppermute | solution.py:22
  3.3 8.7 %collective-permute-start = (f32[8,128]{1,0:T(8,128)S(1)}, f32[8,128]{1,0:T(8,128)S(1)}, u32[]{:S(2)}, u32[]{:S(2)}) collective-permute-start(f32[8,128]{1,0:T(8,128)S(1)} %get-tuple-element.37), channel_id=1, source_target_pairs={{0,1},{1,2},{2,3},{3,4},{4,5},{5,6},{6,7},{7,8},{8,9},{9,10},{10,1... | collective-permute-start | bytes 12296 | tf_op jit(solution)/shard_map/ppermute | solution.py:22
  5.7 6.3 %copy-start.1 = (f32[8,128]{1,0:T(8,128)}, f32[8,128]{1,0:T(8,128)S(1)}, u32[]{:S(2)}) copy-start(f32[8,128]{1,0:T(8,128)S(1)} %collective-permute-done.1.high_ref) | copy-start | bytes 12292
  12.0 0.6 copy-start.2
  33.6 2.7 %copy-start.3 = (f32[8,128]{1,0:T(8,128)S(1)}, f32[8,128]{1,0:T(8,128)}, u32[]{:S(2)}) copy-start(f32[8,128]{1,0:T(8,128)} %get-tuple-element.33) | copy-start | bytes 12292
  33.6 5.1 %collective-permute-start.2 = (f32[8,128]{1,0:T(8,128)}, f32[8,128]{1,0:T(8,128)S(1)}, u32[]{:S(2)}, u32[]{:S(2)}) collective-permute-start(f32[8,128]{1,0:T(8,128)} %get-tuple-element.32), channel_id=1, source_target_pairs={{1,0},{2,1},{3,2},{4,3},{5,4},{6,5},{7,6},{8,7},{9,8},{10,9},{11,1... | collective-permute-start | bytes 12296 | tf_op jit(solution)/shard_map/ppermute | solution.py:22
  36.2 4.9 %collective-permute-start.3 = (f32[8,128]{1,0:T(8,128)S(1)}, f32[8,128]{1,0:T(8,128)S(1)}, u32[]{:S(2)}, u32[]{:S(2)}) collective-permute-start(f32[8,128]{1,0:T(8,128)S(1)} %copy-done.3), channel_id=1, source_target_pairs={{0,1},{1,2},{2,3},{3,4},{4,5},{5,6},{6,7},{7,8},{8,9},{9,10},{10,1... | collective-permute-start | bytes 12296 | tf_op jit(solution)/shard_map/ppermute | solution.py:22
  71.0 3.3 %collective-permute-start.4 = (f32[16,128]{1,0:T(8,128)}, f32[16,128]{1,0:T(8,128)S(1)}, u32[]{:S(2)}, u32[]{:S(2)}) collective-permute-start(f32[16,128]{1,0:T(8,128)} %probe_sum.1.own_ref), channel_id=1, source_target_pairs={{0,1},{1,0},{2,3},{3,2},{4,5},{5,4},{6,7},{7,6},{8,9},{9,8},{10,11... | collective-permute-start | bytes 24584 | tf_op jit(solution)/shard_map/ppermute | solution.py:397
  74.2 0.6 copy-start

commit v4 on v3

--- a/solution.py
+++ b/solution.py
@@ -12,6 +12,7 @@
 LANES = 128
 WIDE = 256
 CORES = 2
+TOGETHER = 8
 
 highest = lax.Precision.HIGHEST
 
@@ -22,16 +23,28 @@
     return lax.ppermute(block, axis, route)
 
 
+def selected(candidates, place, bit):
+    if len(candidates) == 1:
+        return candidates[0]()
+    span = 1 << bit
+    if len(candidates) <= span:
+        return selected(candidates, place, bit - 1)
+    low = selected(candidates[:span], place, bit - 1)
+    high = selected(candidates[span:], place, bit - 1)
+    return jnp.where((place & span) != 0, high, low)
+
+
 def element_kernel(
     low_ref, probes_ref, high_ref, connectivity_ref, sensitivity_ref, weight_ref, prior_ref,
-    images_ref, lower_ref, upper_ref, left_ref, right_ref, total_ref,
+    images_ref, lower_ref, upper_ref, total_ref,
 ):
     probe_count, node_count = probes_ref.shape
     corner_count, element_count = connectivity_ref.shape
     gauss_count = sensitivity_ref.shape[0]
     tiles = node_count // LANES + 2
     blocks = tiles * LANES // WIDE
-    rows = total_ref.shape[0]
+    packed = 2 * probe_count
+    thirds = -(-blocks // 2)
 
     def tile(k):
         if k == 0:
@@ -41,64 +54,100 @@
         return probes_ref[:, (k - 1) * LANES : k * LANES]
 
     total_ref[...] = jnp.zeros_like(total_ref)
-
-    def chunk(step, carry):
-        columns = pl.ds(pl.multiple_of(step * LANES, LANES), LANES)
-        gathered = []
-        nodes = []
-        for corner in range(corner_count):
-            node = jnp.broadcast_to(
-                connectivity_ref[corner : corner + 1, columns], (probe_count, LANES)
+    row = lax.broadcasted_iota(jnp.int32, (WIDE, LANES), 0).astype(jnp.float32).astype(jnp.bfloat16)
+    lower_half = lax.broadcasted_iota(jnp.int32, (packed, LANES), 0) >= probe_count
+    lower_half = jnp.where(lower_half, 1.0, 0.0)
+    one = jnp.ones((WIDE, LANES), jnp.bfloat16)
+    none = jnp.zeros((WIDE, LANES), jnp.bfloat16)
+    zero = jnp.zeros((packed, LANES), jnp.bfloat16)
+    top_bit = (tiles - 1).bit_length() - 1
+
+    def columns_of(step):
+        return pl.ds(pl.multiple_of(step * LANES, LANES), LANES)
+
+    def node_of(corner, step):
+        return jnp.broadcast_to(
+            connectivity_ref[corner : corner + 1, columns_of(step)], (probe_count, LANES)
+        )
+
+    def gather(corner, step):
+        node = node_of(corner, step)
+        lane = node & (LANES - 1)
+        picks = [
+            functools.partial(
+                lambda k, at: jnp.take_along_axis(tile(k), at, axis=1, mode="promise_in_bounds"),
+                k, lane,
             )
-            nodes.append(node)
-            lane = node & (LANES - 1)
-            place = lax.shift_right_logical(node, 7)
-            value = jnp.zeros((probe_count, LANES), jnp.float32)
-            for k in range(tiles):
-                picked = jnp.take_along_axis(tile(k), lane, axis=1, mode="promise_in_bounds")
-                value = jnp.where(place == k, picked, value)
-            gathered.append(value)
+            for k in range(tiles)
+        ]
+        return selected(picks, lax.shift_right_logical(node, 7), top_bit)
+
+    def pull(gathered, step):
+        columns = columns_of(step)
         observed = []
         for gauss in range(gauss_count):
             value = gathered[0] * sensitivity_ref[gauss, 0:1, columns]
             for corner in range(1, corner_count):
                 value = value + gathered[corner] * sensitivity_ref[gauss, corner : corner + 1, columns]
             observed.append(value * weight_ref[gauss : gauss + 1, columns])
+        pulled = []
         for corner in range(corner_count):
             value = observed[0] * sensitivity_ref[0, corner : corner + 1, columns]
             for gauss in range(1, gauss_count):
                 value = value + observed[gauss] * sensitivity_ref[gauss, corner : corner + 1, columns]
-            first = value.astype(jnp.bfloat16).astype(jnp.float32)
-            rest = value - first
-            second = rest.astype(jnp.bfloat16).astype(jnp.float32)
-            third = rest - second
-            node = nodes[corner]
-            place = lax.shift_right_logical(node, 8)
-            zero = jnp.zeros_like(value)
-            pieces = []
-            for k in range(blocks):
-                here = place == k
-                for piece in (first, second, third):
-                    pieces.append(jnp.where(here, piece, zero))
-            while len(pieces) * probe_count < rows:
-                pieces.append(zero)
-            span = slice(corner * LANES, (corner + 1) * LANES)
-            left_ref[:, span] = jnp.concatenate(pieces, axis=0).astype(jnp.bfloat16)
-            lane = jnp.broadcast_to(node[0:1, :] & (WIDE - 1), (WIDE, LANES))
-            row = lax.broadcasted_iota(jnp.int32, (WIDE, LANES), 0)
-            right_ref[:, span] = jnp.where(row == lane, 1.0, 0.0).astype(jnp.bfloat16)
-        total_ref[...] += lax.dot_general(
-            left_ref[...], right_ref[...], (((1,), (1,)), ((), ())),
-            preferred_element_type=jnp.float32,
-        )
-        return carry
-
-    lax.fori_loop(0, element_count // LANES, chunk, 0)
+            pulled.append(value)
+        return tuple(pulled)
+
+    def operands(value, corner, step):
+        first = value.astype(jnp.bfloat16).astype(jnp.float32)
+        rest = value - first
+        second = rest.astype(jnp.bfloat16).astype(jnp.float32)
+        third = rest - second
+        heads = jnp.concatenate([first, second], axis=0).astype(jnp.bfloat16)
+        tails = jnp.concatenate([third, third], axis=0).astype(jnp.bfloat16)
+        node = node_of(corner, step)
+        place = lax.shift_right_logical(node, 8).astype(jnp.float32)
+        place = jnp.concatenate([place, place], axis=0)
+        offset = (place - lower_half).astype(jnp.bfloat16)
+        place = place.astype(jnp.bfloat16)
+        parts = []
+        for k in range(blocks):
+            here = place == jnp.full((packed, LANES), k, jnp.bfloat16)
+            parts.append(jnp.where(here, heads, zero))
+        for k in range(thirds):
+            here = offset == jnp.full((packed, LANES), 2 * k, jnp.bfloat16)
+            parts.append(jnp.where(here, tails, zero))
+        lane = (node & (WIDE - 1)).astype(jnp.float32)
+        lane = jnp.concatenate([lane, lane], axis=0).astype(jnp.bfloat16)
+        lane = jnp.concatenate([lane] * (WIDE // packed), axis=0)
+        return jnp.concatenate(parts, axis=0), jnp.where(row == lane, one, none)
+
+    last = element_count // LANES - 1
+
+    def trip(step, pulled):
+        ahead = jnp.minimum(step + 1, last)
+        gathered = []
+        for group in range(0, corner_count, TOGETHER):
+            left, right = [], []
+            for corner in range(group, group + TOGETHER):
+                gathered.append(gather(corner, ahead))
+                a, b = operands(pulled[corner], corner, step)
+                left.append(a)
+                right.append(b)
+            total_ref[...] += lax.dot_general(
+                jnp.concatenate(left, axis=1), jnp.concatenate(right, axis=1),
+                (((1,), (1,)), ((), ())), preferred_element_type=jnp.float32,
+            )
+        return pull(gathered, ahead)
+
+    pulled = pull([gather(corner, 0) for corner in range(corner_count)], 0)
+    lax.fori_loop(0, last + 1, trip, pulled)
 
     for block in range(blocks):
-        at = block * 3 * probe_count
-        value = total_ref[at + 2 * probe_count : at + 3 * probe_count, :]
-        value = value + total_ref[at + probe_count : at + 2 * probe_count, :]
+        at = block * packed
+        tail = blocks * packed + block * probe_count
+        value = total_ref[tail : tail + probe_count, :]
+        value = value + total_ref[at + probe_count : at + packed, :]
         value = value + total_ref[at : at + probe_count, :]
         for half in range(WIDE // LANES):
             k = block * (WIDE // LANES) + half
@@ -116,7 +165,7 @@
     probe_count, node_count = probes.shape
     corner_count = connectivity.shape[0]
     blocks = (node_count + 2 * HALO) // WIDE
-    rows = -(-blocks * 3 * probe_count // 16) * 16
+    rows = (blocks + -(-blocks // 2)) * 2 * probe_count
     vmem = pl.BlockSpec(memory_space=pltpu.VMEM)
     rim = jax.ShapeDtypeStruct((probe_count, HALO), jnp.float32)
     return pl.pallas_call(
@@ -124,13 +173,16 @@
         out_shape=(jax.ShapeDtypeStruct(probes.shape, jnp.float32), rim, rim),
         in_specs=[vmem] * 7,
         out_specs=(vmem, vmem, vmem),
-        scratch_shapes=[
-            pltpu.VMEM((rows, corner_count * LANES), jnp.bfloat16),
-            pltpu.VMEM((WIDE, corner_count * LANES), jnp.bfloat16),
-            pltpu.VMEM((rows, WIDE), jnp.float32),
-        ],
+        scratch_shapes=[pltpu.VMEM((rows, WIDE), jnp.float32)],
         name="element_images",
     )(low, probes, high, connectivity, sensitivity, obs_weight, prior_weight.reshape(1, -1))
+
+
+def rim_kernel(images_ref, lower_ref, upper_ref, sum_ref):
+    node_count = images_ref.shape[1]
+    sum_ref[...] = images_ref[...]
+    sum_ref[:, :HALO] = images_ref[:, :HALO] + upper_ref[...]
+    sum_ref[:, node_count - HALO :] = images_ref[:, node_count - HALO :] + lower_ref[...]
 
 
 SUBLANES = 8
@@ -420,8 +472,10 @@
     )
     lower_rim = shifted(lower, "space", -1)
     upper_rim = shifted(upper, "space", 1)
-    images = images.at[:, node_count - HALO :].add(lower_rim)
-    images = images.at[:, :HALO].add(upper_rim)
+    images = in_vmem(
+        rim_kernel, "rims", jax.ShapeDtypeStruct(images.shape, jnp.float32),
+        images, lower_rim, upper_rim,
+    )
     scale = math.sqrt(float(node_count * lax.axis_size("space")))
     rows = lax.all_to_all(images, "probe", 1, 0, tiled=True)
     basis, factor = orthonormal(rows, scale)

time: 157 us -> 145 us (0.924)
  Pallas kernels: 50.4 us -> 40.5 us
  other arithmetic: 3.85 us -> 0 us
    pallas_call x1, Pallas kernels: 21 us -> 9.52 us  [element_images(): pl.pallas_call(element_kernel, out_shape=(jax.ShapeDtypeStruct(probes.sha...]
    scatter-add x2 -> x0, other arithmetic: 3.21 us -> none  [the longest x1 1.93 us: on_device(): images = images.at[:, :HALO].add(upper_rim)]
    pallas_call x5 -> x6, Pallas kernels: 29.4 us -> 31 us  [in_vmem(): pl.pallas_call(kernel, out_shape=out_shape, in_specs=[vmem] * len(operand...]
  transfers between devices with their start and end apart: 5 -> 5, of which waited for: 3 -> 3; matrix products, arithmetic and copies ran while one was open for 1% -> 0% of each run, Pallas kernels for 0% -> 0%
where the time goes in v4:
time: 145 us; the launch traced here: 144 us
  blocking collectives  78.7 us (54%)
  Pallas kernels  40.5 us (28%)
  starting transfers between devices  10.5 us (7%)
  waiting for transfers between devices  10.4 us (7%)
  local copies, waits for them, and re-layouts  3.14 us (2%)
    pallas_call x6, Pallas kernels, in_vmem(): pl.pallas_call(kernel, out_shape=out_shape, in_specs=[vmem] * len(operand...  31 us
    all_to_all x1, blocking collectives, orthonormal(): lax.all_to_all(spread, 'space', 0, 0, tiled=True, axis_index_groups=groups)  30.8 us
    all_to_all x1, blocking collectives, orthonormal(): gram = lax.all_to_all(gram, 'probe', 0, 0, tiled=True)  12.2 us
    all_to_all x1, blocking collectives, orthonormal(): whole = lax.all_to_all(whole, 'probe', 0, 0, tiled=True)  12.2 us
    all_to_all x1, blocking collectives, on_device(): rows = lax.all_to_all(images, 'probe', 1, 0, tiled=True)  12.2 us
    all_to_all x1, blocking collectives, on_device(): return (lax.all_to_all(basis, 'probe', 0, 1, tiled=True), factor)  11.5 us
    pallas_call x1, Pallas kernels, element_images(): pl.pallas_call(element_kernel, out_shape=(jax.ShapeDtypeStruct(probes.sha...  9.52 us
    ppermute x4, waiting for transfers between devices, shifted(): return lax.ppermute(block, axis, route)  9.02 us
  transfers between devices with their start and end apart: 5, of which 3 were waited for; matrix products, arithmetic and copies ran while one was open for 0% of the time, Pallas kernels for 0%

profile of v4, /device:TPU:32, one launch (start us, length us, event | category | flops | bytes accessed | tf_op | source)
XLA Modules:
  0.0 144.0 jit_solution(7206061722567173161)
XLA Ops:
  0.6 0.7 fusion
  1.3 1.9 %collective-permute-start.1 = (f32[8,128]{1,0:T(8,128)S(1)}, f32[8,128]{1,0:T(8,128)S(1)}, u32[]{:S(2)}, u32[]{:S(2)}) collective-permute-start(f32[8,128]{1,0:T(8,128)S(1)} %get-tuple-element.12), channel_id=1, source_target_pairs={{1,0},{2,1},{3,2},{4,3},{5,4},{6,5},{7,6},{8,7},{9,8},{10,9},{11,1... | collective-permute-start | bytes 12296 | tf_op jit(solution)/shard_map/ppermute | solution.py:23
  3.3 2.4 %collective-permute-start = (f32[8,128]{1,0:T(8,128)S(1)}, f32[8,128]{1,0:T(8,128)S(1)}, u32[]{:S(2)}, u32[]{:S(2)}) collective-permute-start(f32[8,128]{1,0:T(8,128)S(1)} %get-tuple-element.13), channel_id=1, source_target_pairs={{0,1},{1,2},{2,3},{3,4},{4,5},{5,6},{6,7},{7,8},{8,9},{9,10},{10,1... | collective-permute-start | bytes 12296 | tf_op jit(solution)/shard_map/ppermute | solution.py:23
  5.7 0.0 collective-permute-done.1.high_ref
  5.7 0.0 copy-start.1
  5.7 6.3 %collective-permute-done.low_ref = f32[8,128]{1,0:T(8,128)S(1)} collective-permute-done((f32[8,128]{1,0:T(8,128)S(1)}, f32[8,128]{1,0:T(8,128)S(1)}, u32[]{:S(2)}, u32[]{:S(2)}) %collective-permute-start) | collective-permute-done | bytes 4128 | tf_op jit(solution)/shard_map/ppermute | solution.py:23
  12.0 0.0 copy-start.3
  12.0 0.0 copy-done.1
  12.0 0.6 copy-done.3
  12.6 9.5 %element_images.1 = (f32[8,4096]{1,0:T(8,128)}, f32[8,128]{1,0:T(8,128)}, f32[8,128]{1,0:T(8,128)}) custom-call(f32[8,128]{1,0:T(8,128)} %copy-done.3, f32[8,4096]{1,0:T(8,128)} %probes_ref.1, f32[8,128]{1,0:T(8,128)} %copy-done.1, s32[8,2048]{1,0:T(8,128)} %connectivity_ref.1, f32[8,8,2048]{2,1,0:T(8,128)} %sensitivity_ref.1, f32[8,2048]{1,0:T(8,128)} %weight_ref.1, ...), custom_call_target="tpu_custom_call" | custom-call | tf_op jit(solution)/shard_map/element_images/pallas_call | solution.py:171
  22.1 1.9 %collective-permute-start.2 = (f32[8,128]{1,0:T(8,128)}, f32[8,128]{1,0:T(8,128)S(1)}, u32[]{:S(2)}, u32[]{:S(2)}) collective-permute-start(f32[8,128]{1,0:T(8,128)} %get-tuple-element.8), channel_id=1, source_target_pairs={{1,0},{2,1},{3,2},{4,3},{5,4},{6,5},{7,6},{8,7},{9,8},{10,9},{11,1... | collective-permute-start | bytes 12296 | tf_op jit(solution)/shard_map/ppermute | solution.py:23
  24.0 2.4 %collective-permute-start.3 = (f32[8,128]{1,0:T(8,128)}, f32[8,128]{1,0:T(8,128)S(1)}, u32[]{:S(2)}, u32[]{:S(2)}) collective-permute-start(f32[8,128]{1,0:T(8,128)} %get-tuple-element.9), channel_id=1, source_target_pairs={{0,1},{1,2},{2,3},{3,4},{4,5},{5,6},{6,7},{7,8},{8,9},{9,10},{10,1... | collective-permute-start | bytes 12296 | tf_op jit(solution)/shard_map/ppermute | solution.py:23
  26.5 0.0 collective-permute-done.2.lower_ref
  26.5 0.0 copy-start.2
  26.5 2.7 %collective-permute-done.3.upper_ref = f32[8,128]{1,0:T(8,128)S(1)} collective-permute-done((f32[8,128]{1,0:T(8,128)}, f32[8,128]{1,0:T(8,128)S(1)}, u32[]{:S(2)}, u32[]{:S(2)}) %collective-permute-start.3) | collective-permute-done | bytes 4128 | tf_op jit(solution)/shard_map/ppermute | solution.py:23
  29.2 0.0 copy-start.4
  29.2 0.0 copy-done.2
  29.2 0.6 copy-done.4
  29.8 1.6 %rims.1 = f32[8,4096]{1,0:T(8,128)} custom-call(f32[8,4096]{1,0:T(8,128)} %get-tuple-element.7.images_ref, f32[8,128]{1,0:T(8,128)} %copy-done.2, f32[8,128]{1,0:T(8,128)} %copy-done.4), custom_call_target="tpu_custom_call" | custom-call | tf_op jit(solution)/shard_map/rims/pallas_call | solution.py:427
  31.3 12.2 %all_to_all.53 = f32[8,16,256]{2,0,1:T(8,128)} all-to-all(f32[8,16,256]{2,0,1:T(8,128)} %bitcast.11), channel_id=1, replica_groups=mesh['probe'=16,'space'=32] {'probe'}, dimensions={1} | all-to-all | bytes 262144 | tf_op jit(solution)/shard_map/all_to_all | solution.py:480
  43.5 2.0 %gram.1 = f32[16,16,128]{2,1,0:T(8,128)} custom-call(f32[128,256]{1,0:T(8,128)} %bitcast.9), custom_call_target="tpu_custom_call" | custom-call | tf_op jit(solution)/shard_map/gram/pallas_call | solution.py:427
  45.5 12.2 %all_to_all.54.parts_ref = f32[16,16,128]{2,1,0:T(8,128)} all-to-all(f32[16,16,128]{2,1,0:T(8,128)} %gram.1), channel_id=1, replica_groups=mesh['probe'=16,'space'=32] {'probe'}, dimensions={0} | all-to-all | bytes 262144 | tf_op jit(solution)/shard_map/all_to_all | solution.py:447
  57.7 1.5 %probe_sum.1.own_ref = f32[16,128]{1,0:T(8,128)} custom-call(f32[16,16,128]{2,1,0:T(8,128)} %all_to_all.54.parts_ref), custom_call_target="tpu_custom_call" | custom-call | tf_op jit(solution)/shard_map/probe_sum/pallas_call | solution.py:427
  59.2 1.9 %collective-permute-start.4 = (f32[16,128]{1,0:T(8,128)}, f32[16,128]{1,0:T(8,128)S(1)}, u32[]{:S(2)}, u32[]{:S(2)}) collective-permute-start(f32[16,128]{1,0:T(8,128)} %probe_sum.1.own_ref), channel_id=1, source_target_pairs={{0,1},{1,0},{2,3},{3,2},{4,5},{5,4},{6,7},{7,6},{8,9},{9,8},{10,11... | collective-permute-start | bytes 24584 | tf_op jit(solution)/shard_map/ppermute | solution.py:449
  61.1 1.3 collective-permute-done.4.other_ref
  62.5 0.0 copy-start
  62.5 0.6 copy-done
  63.1 1.4 core_sum.1
  64.5 30.8 %all_to_all.55.parts_ref = f32[16,16,128]{2,1,0:T(8,128)} all-to-all(f32[16,16,128]{2,1,0:T(8,128)} %core_sum.1), channel_id=1, replica_groups={{0,2,4,6,8,10,12,14,16,18,20,22,24,26,28,30},{1,3,5,7,9,11,13,15,17,19,..., dimensions={0} | all-to-all | bytes 262144 | tf_op jit(solution)/shard_map/all_to_all | solution.py:452
  95.3 1.6 %space_sum.1 = f32[16,16,128]{2,1,0:T(8,128)} custom-call(f32[16,16,128]{2,1,0:T(8,128)} %all_to_all.55.parts_ref), custom_call_target="tpu_custom_call" | custom-call | tf_op jit(solution)/shard_map/space_sum/pallas_call | solution.py:427
  96.9 12.2 %all_to_all.56.pair_ref = f32[16,16,128]{2,1,0:T(8,128)} all-to-all(f32[16,16,128]{2,1,0:T(8,128)} %space_sum.1), channel_id=1, replica_groups=mesh['probe'=16,'space'=32] {'probe'}, dimensions={0} | all-to-all | bytes 262144 | tf_op jit(solution)/shard_map/all_to_all | solution.py:454
  109.0 22.9 %basis.1 = (f32[128,256]{1,0:T(8,128)}, f32[128,128]{1,0:T(8,128)}) custom-call(f32[16,16,128]{2,1,0:T(8,128)} %all_to_all.56.pair_ref, f32[128,256]{1,0:T(8,128)} %bitcast.10), custom_call_target="tpu_custom_call" | custom-call | tf_op jit(solution)/shard_map/basis/pallas_call | solution.py:427
  131.9 11.5 %all_to_all.57 = f32[16,8,256]{2,1,0:T(8,128)S(1)} all-to-all(f32[16,8,256]{2,1,0:T(8,128)} %bitcast.13), channel_id=1, replica_groups=mesh['probe'=16,'space'=32] {'probe'}, dimensions={0} | all-to-all | bytes 262144 | tf_op jit(solution)/shard_map/all_to_all | solution.py:482
  143.3 0.7 copy.8
Async XLA Ops:
  1.3 4.3 %collective-permute-start.1 = (f32[8,128]{1,0:T(8,128)S(1)}, f32[8,128]{1,0:T(8,128)S(1)}, u32[]{:S(2)}, u32[]{:S(2)}) collective-permute-start(f32[8,128]{1,0:T(8,128)S(1)} %get-tuple-element.12), channel_id=1, source_target_pairs={{1,0},{2,1},{3,2},{4,3},{5,4},{6,5},{7,6},{8,7},{9,8},{10,9},{11,1... | collective-permute-start | bytes 12296 | tf_op jit(solution)/shard_map/ppermute | solution.py:23
  3.3 8.7 %collective-permute-start = (f32[8,128]{1,0:T(8,128)S(1)}, f32[8,128]{1,0:T(8,128)S(1)}, u32[]{:S(2)}, u32[]{:S(2)}) collective-permute-start(f32[8,128]{1,0:T(8,128)S(1)} %get-tuple-element.13), channel_id=1, source_target_pairs={{0,1},{1,2},{2,3},{3,4},{4,5},{5,6},{6,7},{7,8},{8,9},{9,10},{10,1... | collective-permute-start | bytes 12296 | tf_op jit(solution)/shard_map/ppermute | solution.py:23
  5.7 6.3 %copy-start.1 = (f32[8,128]{1,0:T(8,128)}, f32[8,128]{1,0:T(8,128)S(1)}, u32[]{:S(2)}) copy-start(f32[8,128]{1,0:T(8,128)S(1)} %collective-permute-done.1.high_ref) | copy-start | bytes 12292
  12.0 0.6 copy-start.3
  22.1 4.3 %collective-permute-start.2 = (f32[8,128]{1,0:T(8,128)}, f32[8,128]{1,0:T(8,128)S(1)}, u32[]{:S(2)}, u32[]{:S(2)}) collective-permute-start(f32[8,128]{1,0:T(8,128)} %get-tuple-element.8), channel_id=1, source_target_pairs={{1,0},{2,1},{3,2},{4,3},{5,4},{6,5},{7,6},{8,7},{9,8},{10,9},{11,1... | collective-permute-start | bytes 12296 | tf_op jit(solution)/shard_map/ppermute | solution.py:23
  24.0 5.1 %collective-permute-start.3 = (f32[8,128]{1,0:T(8,128)}, f32[8,128]{1,0:T(8,128)S(1)}, u32[]{:S(2)}, u32[]{:S(2)}) collective-permute-start(f32[8,128]{1,0:T(8,128)} %get-tuple-element.9), channel_id=1, source_target_pairs={{0,1},{1,2},{2,3},{3,4},{4,5},{5,6},{6,7},{7,8},{8,9},{9,10},{10,1... | collective-permute-start | bytes 12296 | tf_op jit(solution)/shard_map/ppermute | solution.py:23
  26.5 2.7 %copy-start.2 = (f32[8,128]{1,0:T(8,128)}, f32[8,128]{1,0:T(8,128)S(1)}, u32[]{:S(2)}) copy-start(f32[8,128]{1,0:T(8,128)S(1)} %collective-permute-done.2.lower_ref) | copy-start | bytes 12292
  29.2 0.6 copy-start.4
  59.2 3.3 %collective-permute-start.4 = (f32[16,128]{1,0:T(8,128)}, f32[16,128]{1,0:T(8,128)S(1)}, u32[]{:S(2)}, u32[]{:S(2)}) collective-permute-start(f32[16,128]{1,0:T(8,128)} %probe_sum.1.own_ref), channel_id=1, source_target_pairs={{0,1},{1,0},{2,3},{3,2},{4,5},{5,4},{6,7},{7,6},{8,9},{9,8},{10,11... | collective-permute-start | bytes 24584 | tf_op jit(solution)/shard_map/ppermute | solution.py:449
  62.5 0.6 copy-start

commit v5 on v4

--- a/solution.py
+++ b/solution.py
@@ -178,15 +178,9 @@
     )(low, probes, high, connectivity, sensitivity, obs_weight, prior_weight.reshape(1, -1))
 
 
-def rim_kernel(images_ref, lower_ref, upper_ref, sum_ref):
-    node_count = images_ref.shape[1]
-    sum_ref[...] = images_ref[...]
-    sum_ref[:, :HALO] = images_ref[:, :HALO] + upper_ref[...]
-    sum_ref[:, node_count - HALO :] = images_ref[:, node_count - HALO :] + lower_ref[...]
-
-
 SUBLANES = 8
 GROUP = 2
+PART = 32
 SLICE = 2.0**-8
 PROBE_SLICES = 4
 GRAM_SLICES = 5
@@ -342,10 +336,10 @@
     return done, pivots
 
 
-def triangles(gram, tile_ref, pivot_ref):
-    size = gram.shape[0]
+def eliminate(work_ref, tile_ref, pivot_ref, upper_ref, inverse_ref):
+    size = work_ref.shape[0]
     count = size // SUBLANES
-    tiles = [gram[k * SUBLANES : (k + 1) * SUBLANES, :] for k in range(count)]
+    tiles = [work_ref[k * SUBLANES : (k + 1) * SUBLANES, :] for k in range(count)]
 
     def block(step, tiles):
         tiles = list(tiles)
@@ -367,16 +361,63 @@
     root = lax.rsqrt(pivot)
     root = root * (1.5 - 0.5 * pivot * root * root)
     scaled = tile * root
-    upper = jnp.where(lane > row, scaled, jnp.where(lane == row, pivot * root, 0.0))
-    inverse = jnp.where(lane < row, scaled, jnp.where(lane == row, root, 0.0))
-    return upper, inverse
-
-
-def exact(a, b):
-    return jnp.dot(a, b, precision=highest, preferred_element_type=jnp.float32)
-
-
-def basis_kernel(scale, pair_ref, rows_ref, basis_ref, factor_ref, tile_ref, pivot_ref):
+    upper_ref[...] = jnp.where(lane > row, scaled, jnp.where(lane == row, pivot * root, 0.0))
+    inverse_ref[...] = jnp.where(lane < row, scaled, jnp.where(lane == row, root, 0.0))
+
+
+def second_gram(work_ref, low_ref, inverse_ref, gram_ref, slice_ref, lower_ref, one_ref, two_ref):
+    size = work_ref.shape[0]
+
+    def part(step):
+        return pl.ds(pl.multiple_of(step * PART, PART), PART)
+
+    def shifted_part(a, step):
+        return pl.ds(pl.multiple_of(a * size + step * PART, PART), PART)
+
+    def four_where(value):
+        return jnp.where(jnp.max(jnp.abs(value), axis=1, keepdims=True) > 0.0, 4.0, 8.0)
+
+    def cut(step, carry):
+        high, low, inverse = work_ref[part(step), :], low_ref[part(step), :], inverse_ref[part(step), :]
+        for a, piece in enumerate(sliced(high, four_where(high), GRAM_SLICES, late=low, late_at=3)):
+            gram_ref[shifted_part(a, step), :] = piece.astype(jnp.bfloat16)
+        bound = bound_of(jnp.max(jnp.abs(inverse), axis=1, keepdims=True))
+        for a, piece in enumerate(sliced(inverse, bound, INVERSE_SLICES)):
+            slice_ref[shifted_part(a, step), :] = piece.astype(jnp.bfloat16)
+        return carry
+
+    def lower(step, carry):
+        high, low = add_levels(
+            lambda a, b: one_ref[shifted_part(a, step), b * size : (b + 1) * size],
+            GRAM_SLICES, INVERSE_SLICES, 6,
+        )
+        for b, piece in enumerate(sliced(high, four_where(high), FIRST_SLICES, late=low, late_at=3)):
+            lower_ref[part(step), b * size : (b + 1) * size] = piece.astype(jnp.bfloat16)
+        return carry
+
+    def total(step, carry):
+        high, low = add_levels(
+            lambda a, b: two_ref[shifted_part(a, step), b * size : (b + 1) * size],
+            INVERSE_SLICES, FIRST_SLICES, 5,
+        )
+        work_ref[part(step), :] = high + low
+        return carry
+
+    parts = size // PART
+    lax.fori_loop(0, parts, cut, 0)
+    one_ref[...] = lax.dot_general(
+        gram_ref[...], slice_ref[...], (((1,), (1,)), ((), ())), preferred_element_type=jnp.float32
+    )
+    lax.fori_loop(0, parts, lower, 0)
+    two_ref[...] = jnp.dot(slice_ref[...], lower_ref[...], preferred_element_type=jnp.float32)
+    lax.fori_loop(0, parts, total, 0)
+
+
+def basis_kernel(
+    scale, pair_ref, rows_ref, basis_ref, factor_ref,
+    work_ref, low_ref, tile_ref, pivot_ref, factors_ref, values_ref,
+    gram_ref, slice_ref, lower_ref, one_ref, two_ref,
+):
     parts, double, size = pair_ref.shape
     count = double // 2
     high = jnp.concatenate([pair_ref[k, :count, :] for k in range(parts)], axis=0)
@@ -388,37 +429,53 @@
     across = jnp.floor(jnp.log(jnp.max(diagonal, axis=0, keepdims=True)) * (0.5 / math.log(2.0)))
     shrink = power_of_two(-down)
     shrink_across = power_of_two(-across)
-    four = jnp.where(shrink > 0.0, 4.0, 8.0)
-    high = high * shrink * shrink_across
-    low = low * shrink * shrink_across
-
-    upper_first, inverse_first = triangles(high, tile_ref, pivot_ref)
-
-    gram_slices = sliced(high, four, GRAM_SLICES, late=low, late_at=3)
-    bound = bound_of(jnp.max(jnp.abs(inverse_first), axis=1, keepdims=True))
-    inverse_slices = sliced(inverse_first, bound, INVERSE_SLICES)
-    gram_stack = jnp.concatenate(gram_slices, axis=0).astype(jnp.bfloat16)
-    inverse_stack = jnp.concatenate(inverse_slices, axis=0).astype(jnp.bfloat16)
-    products = lax.dot_general(
-        gram_stack, inverse_stack, (((1,), (1,)), ((), ())), preferred_element_type=jnp.float32
-    )
-    lower_high, lower_low = add_levels(
-        block_reader(products, size), GRAM_SLICES, INVERSE_SLICES, 6
-    )
-    lower_slices = sliced(lower_high, four, FIRST_SLICES, late=lower_low, late_at=3)
-    lower_stack = jnp.concatenate(lower_slices, axis=1).astype(jnp.bfloat16)
-    products = jnp.dot(inverse_stack, lower_stack, preferred_element_type=jnp.float32)
-    gram_second, rest = add_levels(
-        block_reader(products, size), INVERSE_SLICES, FIRST_SLICES, 5
-    )
-    gram_second = gram_second + rest
-
-    upper_second, inverse_second = triangles(gram_second, tile_ref, pivot_ref)
-    basis_first = exact(inverse_first, rows_ref[...] * shrink)
-    basis = exact(inverse_second, basis_first)
-    basis_ref[...] = basis * scale
-    factor = exact(upper_second, upper_first)
-    factor_ref[...] = factor * (power_of_two(across) * (1.0 / scale))
+    work_ref[...] = high * shrink * shrink_across
+    low_ref[...] = low * shrink * shrink_across
+    grow = power_of_two(across) * (1.0 / scale)
+    for k in range(2):
+        values_ref[k] = rows_ref[:, k * size : (k + 1) * size] * shrink
+
+    def each(step, carry):
+        eliminate(work_ref, tile_ref, pivot_ref, factors_ref.at[2 + step], factors_ref.at[step])
+
+        @pl.when(step == 0)
+        def _():
+            values_ref[4] = factors_ref[2]
+            second_gram(
+                work_ref, low_ref, factors_ref.at[0], gram_ref, slice_ref, lower_ref, one_ref, two_ref
+            )
+
+        return carry
+
+    lax.fori_loop(0, 2, each, 0)
+
+    def multiply(step, carry):
+        late = (step >= 2).astype(jnp.int32)
+        last = (step >= 4).astype(jnp.int32)
+        values_ref[step + 2 + late] = jnp.dot(
+            factors_ref[late + 2 * last], values_ref[step],
+            precision=highest, preferred_element_type=jnp.float32,
+        )
+        return carry
+
+    lax.fori_loop(0, 5, multiply, 0)
+    for k in range(2):
+        basis_ref[:, k * size : (k + 1) * size] = values_ref[5 + k] * scale
+    factor_ref[...] = values_ref[7] * grow
+
+
+def basis_scratch(size):
+    square = pltpu.VMEM((size, size), jnp.float32)
+    return (
+        square, square, square, square,
+        pltpu.VMEM((4, size, size), jnp.float32),
+        pltpu.VMEM((8, size, size), jnp.float32),
+        pltpu.VMEM((GRAM_SLICES * size, size), jnp.bfloat16),
+        pltpu.VMEM((INVERSE_SLICES * size, size), jnp.bfloat16),
+        pltpu.VMEM((size, FIRST_SLICES * size), jnp.bfloat16),
+        pltpu.VMEM((GRAM_SLICES * size, INVERSE_SLICES * size), jnp.float32),
+        pltpu.VMEM((INVERSE_SLICES * size, FIRST_SLICES * size), jnp.float32),
+    )
 
 
 def in_vmem(kernel, name, out_shape, *operands, scratch=()):
@@ -459,7 +516,7 @@
             jax.ShapeDtypeStruct((size, size), jnp.float32),
         ),
         whole, rows,
-        scratch=(pltpu.VMEM((size, size), jnp.float32),) * 2,
+        scratch=basis_scratch(size),
     )
 
 
@@ -472,9 +529,13 @@
     )
     lower_rim = shifted(lower, "space", -1)
     upper_rim = shifted(upper, "space", 1)
-    images = in_vmem(
-        rim_kernel, "rims", jax.ShapeDtypeStruct(images.shape, jnp.float32),
-        images, lower_rim, upper_rim,
+    images = jnp.concatenate(
+        [
+            images[:, :HALO] + upper_rim,
+            images[:, HALO : node_count - HALO],
+            images[:, node_count - HALO :] + lower_rim,
+        ],
+        axis=1,
     )
     scale = math.sqrt(float(node_count * lax.axis_size("space")))
     rows = lax.all_to_all(images, "probe", 1, 0, tiled=True)

time: 145 us -> 145 us (level)
  waiting for transfers between devices: 10.4 us -> 8.27 us
    ppermute x4, waiting for transfers between devices: 9.02 us -> 6.92 us  [shifted(): return lax.ppermute(block, axis, route)]
    pallas_call x6 -> x5, Pallas kernels: 31 us -> 30.8 us  [in_vmem(): pl.pallas_call(kernel, out_shape=out_shape, in_specs=[vmem] * len(operand...]
  transfers between devices with their start and end apart: 5 -> 5, of which waited for: 3 -> 3; matrix products, arithmetic and copies ran while one was open for 0% -> 1% of each run, Pallas kernels for 0% -> 0%
where the time goes in v5:
time: 145 us; the launch traced here: 144 us
  blocking collectives  78.5 us (54%)
  Pallas kernels  40.3 us (28%)
  starting transfers between devices  11.8 us (8%)
  waiting for transfers between devices  8.27 us (6%)
  local copies, waits for them, and re-layouts  3.46 us (2%)
    all_to_all x1, blocking collectives, orthonormal(): lax.all_to_all(spread, 'space', 0, 0, tiled=True, axis_index_groups=groups)  31.2 us
    pallas_call x5, Pallas kernels, in_vmem(): pl.pallas_call(kernel, out_shape=out_shape, in_specs=[vmem] * len(operand...  30.8 us
    all_to_all x1, blocking collectives, orthonormal(): gram = lax.all_to_all(gram, 'probe', 0, 0, tiled=True)  12.3 us
    all_to_all x1, blocking collectives, orthonormal(): whole = lax.all_to_all(whole, 'probe', 0, 0, tiled=True)  12.1 us
    all_to_all x1, blocking collectives, on_device(): return (lax.all_to_all(basis, 'probe', 0, 1, tiled=True), factor)  11.5 us
    all_to_all x1, blocking collectives, on_device(): rows = lax.all_to_all(images, 'probe', 1, 0, tiled=True)  11.4 us
    ppermute x4, starting transfers between devices, shifted(): return lax.ppermute(block, axis, route)  9.86 us
    pallas_call x1, Pallas kernels, element_images(): pl.pallas_call(element_kernel, out_shape=(jax.ShapeDtypeStruct(probes.sha...  9.52 us
  transfers between devices with their start and end apart: 5, of which 3 were waited for; matrix products, arithmetic and copies ran while one was open for 1% of the time, Pallas kernels for 0%

profile of v5, /device:TPU:32, one launch (start us, length us, event | category | flops | bytes accessed | tf_op | source)
XLA Modules:
  0.0 143.7 jit_solution(724451461948325155)
XLA Ops:
  0.6 0.7 fusion
  1.3 1.9 %collective-permute-start.1 = (f32[8,128]{1,0:T(8,128)S(1)}, f32[8,128]{1,0:T(8,128)S(1)}, u32[]{:S(2)}, u32[]{:S(2)}) collective-permute-start(f32[8,128]{1,0:T(8,128)S(1)} %get-tuple-element.14), channel_id=1, source_target_pairs={{1,0},{2,1},{3,2},{4,3},{5,4},{6,5},{7,6},{8,7},{9,8},{10,9},{11,1... | collective-permute-start | bytes 12296 | tf_op jit(solution)/shard_map/ppermute | solution.py:23
  3.3 2.4 %collective-permute-start = (f32[8,128]{1,0:T(8,128)S(1)}, f32[8,128]{1,0:T(8,128)S(1)}, u32[]{:S(2)}, u32[]{:S(2)}) collective-permute-start(f32[8,128]{1,0:T(8,128)S(1)} %get-tuple-element.15), channel_id=1, source_target_pairs={{0,1},{1,2},{2,3},{3,4},{4,5},{5,6},{6,7},{7,8},{8,9},{9,10},{10,1... | collective-permute-start | bytes 12296 | tf_op jit(solution)/shard_map/ppermute | solution.py:23
  5.7 0.0 collective-permute-done.1.high_ref
  5.7 0.0 copy-start.1
  5.7 6.3 %collective-permute-done.low_ref = f32[8,128]{1,0:T(8,128)S(1)} collective-permute-done((f32[8,128]{1,0:T(8,128)S(1)}, f32[8,128]{1,0:T(8,128)S(1)}, u32[]{:S(2)}, u32[]{:S(2)}) %collective-permute-start) | collective-permute-done | bytes 4128 | tf_op jit(solution)/shard_map/ppermute | solution.py:23
  12.0 0.0 copy-start.2
  12.0 0.0 copy-done.1
  12.0 0.6 copy-done.2
  12.6 9.5 %element_images.1 = (f32[8,4096]{1,0:T(8,128)}, f32[8,128]{1,0:T(8,128)}, f32[8,128]{1,0:T(8,128)}) custom-call(f32[8,128]{1,0:T(8,128)} %copy-done.2, f32[8,4096]{1,0:T(8,128)} %probes_ref.1, f32[8,128]{1,0:T(8,128)} %copy-done.1, s32[8,2048]{1,0:T(8,128)} %connectivity_ref.1, f32[8,8,2048]{2,1,0:T(8,128)} %sensitivity_ref.1, f32[8,2048]{1,0:T(8,128)} %weight_ref.1, ...), custom_call_target="tpu_custom_call" | custom-call | tf_op jit(solution)/shard_map/element_images/pallas_call | solution.py:171
  22.1 1.9 %collective-permute-start.2 = (f32[8,128]{1,0:T(8,128)}, f32[8,128]{1,0:T(8,128)S(1)}, u32[]{:S(2)}, u32[]{:S(2)}) collective-permute-start(f32[8,128]{1,0:T(8,128)} %get-tuple-element.8), channel_id=1, source_target_pairs={{0,1},{1,2},{2,3},{3,4},{4,5},{5,6},{6,7},{7,8},{8,9},{9,10},{10,1... | collective-permute-start | bytes 12296 | tf_op jit(solution)/shard_map/ppermute | solution.py:23
  24.0 3.6 %collective-permute-start.3 = (f32[8,128]{1,0:T(8,128)}, f32[8,128]{1,0:T(8,128)S(1)}, u32[]{:S(2)}, u32[]{:S(2)}) collective-permute-start(f32[8,128]{1,0:T(8,128)} %get-tuple-element.9), channel_id=1, source_target_pairs={{1,0},{2,1},{3,2},{4,3},{5,4},{6,5},{7,6},{8,7},{9,8},{10,9},{11,1... | collective-permute-start | bytes 12296 | tf_op jit(solution)/shard_map/ppermute | solution.py:23
  27.7 0.9 slice.18
  28.6 0.0 collective-permute-done.2
  28.6 0.6 collective-permute-done.3
  29.2 0.7 slice_add_fusion.1
  29.9 11.4 %all_to_all.53 = f32[8,16,256]{2,0,1:T(8,128)} all-to-all(f32[8,16,256]{2,0,1:T(8,128)S(1)} %bitcast.11), channel_id=1, replica_groups=mesh['probe'=16,'space'=32] {'probe'}, dimensions={1} | all-to-all | bytes 262144 | tf_op jit(solution)/shard_map/all_to_all | solution.py:541
  41.3 2.0 %gram.1 = f32[16,16,128]{2,1,0:T(8,128)} custom-call(f32[128,256]{1,0:T(8,128)} %bitcast.9), custom_call_target="tpu_custom_call" | custom-call | tf_op jit(solution)/shard_map/gram/pallas_call | solution.py:484
  43.3 12.3 %all_to_all.54.parts_ref = f32[16,16,128]{2,1,0:T(8,128)} all-to-all(f32[16,16,128]{2,1,0:T(8,128)} %gram.1), channel_id=1, replica_groups=mesh['probe'=16,'space'=32] {'probe'}, dimensions={0} | all-to-all | bytes 262144 | tf_op jit(solution)/shard_map/all_to_all | solution.py:504
  55.6 1.5 %probe_sum.1.own_ref = f32[16,128]{1,0:T(8,128)} custom-call(f32[16,16,128]{2,1,0:T(8,128)} %all_to_all.54.parts_ref), custom_call_target="tpu_custom_call" | custom-call | tf_op jit(solution)/shard_map/probe_sum/pallas_call | solution.py:484
  57.2 1.9 %collective-permute-start.4 = (f32[16,128]{1,0:T(8,128)}, f32[16,128]{1,0:T(8,128)S(1)}, u32[]{:S(2)}, u32[]{:S(2)}) collective-permute-start(f32[16,128]{1,0:T(8,128)} %probe_sum.1.own_ref), channel_id=1, source_target_pairs={{0,1},{1,0},{2,3},{3,2},{4,5},{5,4},{6,7},{7,6},{8,9},{9,8},{10,11... | collective-permute-start | bytes 24584 | tf_op jit(solution)/shard_map/ppermute | solution.py:506
  59.1 1.3 collective-permute-done.4.other_ref
  60.4 0.0 copy-start
  60.4 0.6 copy-done
  61.0 1.4 core_sum.1
  62.4 31.2 %all_to_all.55.parts_ref = f32[16,16,128]{2,1,0:T(8,128)} all-to-all(f32[16,16,128]{2,1,0:T(8,128)} %core_sum.1), channel_id=1, replica_groups={{0,2,4,6,8,10,12,14,16,18,20,22,24,26,28,30},{1,3,5,7,9,11,13,15,17,19,..., dimensions={0} | all-to-all | bytes 262144 | tf_op jit(solution)/shard_map/all_to_all | solution.py:509
  93.6 1.6 %space_sum.1 = f32[16,16,128]{2,1,0:T(8,128)} custom-call(f32[16,16,128]{2,1,0:T(8,128)} %all_to_all.55.parts_ref), custom_call_target="tpu_custom_call" | custom-call | tf_op jit(solution)/shard_map/space_sum/pallas_call | solution.py:484
  95.2 12.1 %all_to_all.56.pair_ref = f32[16,16,128]{2,1,0:T(8,128)} all-to-all(f32[16,16,128]{2,1,0:T(8,128)} %space_sum.1), channel_id=1, replica_groups=mesh['probe'=16,'space'=32] {'probe'}, dimensions={0} | all-to-all | bytes 262144 | tf_op jit(solution)/shard_map/all_to_all | solution.py:511
  107.4 24.2 %basis.1 = (f32[128,256]{1,0:T(8,128)}, f32[128,128]{1,0:T(8,128)}) custom-call(f32[16,16,128]{2,1,0:T(8,128)} %all_to_all.56.pair_ref, f32[128,256]{1,0:T(8,128)} %bitcast.10), custom_call_target="tpu_custom_call" | custom-call | tf_op jit(solution)/shard_map/basis/pallas_call | solution.py:484
  131.6 11.5 %all_to_all.57 = f32[16,8,256]{2,1,0:T(8,128)S(1)} all-to-all(f32[16,8,256]{2,1,0:T(8,128)} %bitcast.13), channel_id=1, replica_groups=mesh['probe'=16,'space'=32] {'probe'}, dimensions={0} | all-to-all | bytes 262144 | tf_op jit(solution)/shard_map/all_to_all | solution.py:543
  143.1 0.7 copy.8
  (1 shorter events, 0.0 us)
Async XLA Ops:
  1.3 4.3 %collective-permute-start.1 = (f32[8,128]{1,0:T(8,128)S(1)}, f32[8,128]{1,0:T(8,128)S(1)}, u32[]{:S(2)}, u32[]{:S(2)}) collective-permute-start(f32[8,128]{1,0:T(8,128)S(1)} %get-tuple-element.14), channel_id=1, source_target_pairs={{1,0},{2,1},{3,2},{4,3},{5,4},{6,5},{7,6},{8,7},{9,8},{10,9},{11,1... | collective-permute-start | bytes 12296 | tf_op jit(solution)/shard_map/ppermute | solution.py:23
  3.3 8.7 %collective-permute-start = (f32[8,128]{1,0:T(8,128)S(1)}, f32[8,128]{1,0:T(8,128)S(1)}, u32[]{:S(2)}, u32[]{:S(2)}) collective-permute-start(f32[8,128]{1,0:T(8,128)S(1)} %get-tuple-element.15), channel_id=1, source_target_pairs={{0,1},{1,2},{2,3},{3,4},{4,5},{5,6},{6,7},{7,8},{8,9},{9,10},{10,1... | collective-permute-start | bytes 12296 | tf_op jit(solution)/shard_map/ppermute | solution.py:23
  5.7 6.3 %copy-start.1 = (f32[8,128]{1,0:T(8,128)}, f32[8,128]{1,0:T(8,128)S(1)}, u32[]{:S(2)}) copy-start(f32[8,128]{1,0:T(8,128)S(1)} %collective-permute-done.1.high_ref) | copy-start | bytes 12292
  12.0 0.6 copy-start.2
  22.1 6.5 %collective-permute-start.2 = (f32[8,128]{1,0:T(8,128)}, f32[8,128]{1,0:T(8,128)S(1)}, u32[]{:S(2)}, u32[]{:S(2)}) collective-permute-start(f32[8,128]{1,0:T(8,128)} %get-tuple-element.8), channel_id=1, source_target_pairs={{0,1},{1,2},{2,3},{3,4},{4,5},{5,6},{6,7},{7,8},{8,9},{9,10},{10,1... | collective-permute-start | bytes 12296 | tf_op jit(solution)/shard_map/ppermute | solution.py:23
  24.0 5.2 %collective-permute-start.3 = (f32[8,128]{1,0:T(8,128)}, f32[8,128]{1,0:T(8,128)S(1)}, u32[]{:S(2)}, u32[]{:S(2)}) collective-permute-start(f32[8,128]{1,0:T(8,128)} %get-tuple-element.9), channel_id=1, source_target_pairs={{1,0},{2,1},{3,2},{4,3},{5,4},{6,5},{7,6},{8,7},{9,8},{10,9},{11,1... | collective-permute-start | bytes 12296 | tf_op jit(solution)/shard_map/ppermute | solution.py:23
  57.2 3.3 %collective-permute-start.4 = (f32[16,128]{1,0:T(8,128)}, f32[16,128]{1,0:T(8,128)S(1)}, u32[]{:S(2)}, u32[]{:S(2)}) collective-permute-start(f32[16,128]{1,0:T(8,128)} %probe_sum.1.own_ref), channel_id=1, source_target_pairs={{0,1},{1,0},{2,3},{3,2},{4,5},{5,4},{6,7},{7,6},{8,9},{9,8},{10,11... | collective-permute-start | bytes 24584 | tf_op jit(solution)/shard_map/ppermute | solution.py:506
  60.4 0.6 copy-start

commit v6 on v4

--- a/solution.py
+++ b/solution.py
@@ -186,7 +186,8 @@
 
 
 SUBLANES = 8
-GROUP = 2
+GROUP = 8
+STAGES = 8
 SLICE = 2.0**-8
 PROBE_SLICES = 4
 GRAM_SLICES = 5
@@ -358,9 +359,10 @@
         tiles = [pltpu.roll(tile, size - SUBLANES, 1) for tile in tiles]
         return tuple(tiles[1:] + tiles[:1])
 
-    half = count // 2
-    tiles = lax.fori_loop(0, half, block, tuple(tiles))
-    lax.fori_loop(half, count, block, tuple(tiles[:half]))
+    each = count // STAGES
+    for stage in range(STAGES):
+        tiles = lax.fori_loop(stage * each, (stage + 1) * each, block, tuple(tiles))
+        tiles = tiles[: len(tiles) - each]
     tile, pivot = tile_ref[...], pivot_ref[...]
     lane = lax.broadcasted_iota(jnp.int32, tile.shape, 1)
     row = lax.broadcasted_iota(jnp.int32, tile.shape, 0)

time: 145 us -> 137 us (0.945)
  Pallas kernels: 40.5 us -> 32.5 us
    pallas_call x6, Pallas kernels: 31 us -> 23 us  [in_vmem(): pl.pallas_call(kernel, out_shape=out_shape, in_specs=[vmem] * len(operand...]
where the time goes in v6:
time: 137 us; the launch traced here: 136 us
  blocking collectives  78.7 us (57%)
  Pallas kernels  32.5 us (24%)
  starting transfers between devices  10.5 us (8%)
  waiting for transfers between devices  10.4 us (8%)
  local copies, waits for them, and re-layouts  3.14 us (2%)
    all_to_all x1, blocking collectives, orthonormal(): lax.all_to_all(spread, 'space', 0, 0, tiled=True, axis_index_groups=groups)  30.8 us
    pallas_call x6, Pallas kernels, in_vmem(): pl.pallas_call(kernel, out_shape=out_shape, in_specs=[vmem] * len(operand...  23 us
    all_to_all x1, blocking collectives, orthonormal(): gram = lax.all_to_all(gram, 'probe', 0, 0, tiled=True)  12.2 us
    all_to_all x1, blocking collectives, orthonormal(): whole = lax.all_to_all(whole, 'probe', 0, 0, tiled=True)  12.2 us
    all_to_all x1, blocking collectives, on_device(): rows = lax.all_to_all(images, 'probe', 1, 0, tiled=True)  12.2 us
    all_to_all x1, blocking collectives, on_device(): return (lax.all_to_all(basis, 'probe', 0, 1, tiled=True), factor)  11.5 us
    pallas_call x1, Pallas kernels, element_images(): pl.pallas_call(element_kernel, out_shape=(jax.ShapeDtypeStruct(probes.sha...  9.52 us
    ppermute x4, waiting for transfers between devices, shifted(): return lax.ppermute(block, axis, route)  9.02 us
  transfers between devices with their start and end apart: 5, of which 3 were waited for; matrix products, arithmetic and copies ran while one was open for 0% of the time, Pallas kernels for 0%

profile of v6, /device:TPU:32, one launch (start us, length us, event | category | flops | bytes accessed | tf_op | source)
XLA Modules:
  0.0 136.0 jit_solution(11449615224013574805)
XLA Ops:
  0.6 0.7 fusion
  1.3 1.9 %collective-permute-start.1 = (f32[8,128]{1,0:T(8,128)S(1)}, f32[8,128]{1,0:T(8,128)S(1)}, u32[]{:S(2)}, u32[]{:S(2)}) collective-permute-start(f32[8,128]{1,0:T(8,128)S(1)} %get-tuple-element.12), channel_id=1, source_target_pairs={{1,0},{2,1},{3,2},{4,3},{5,4},{6,5},{7,6},{8,7},{9,8},{10,9},{11,1... | collective-permute-start | bytes 12296 | tf_op jit(solution)/shard_map/ppermute | solution.py:23
  3.3 2.4 %collective-permute-start = (f32[8,128]{1,0:T(8,128)S(1)}, f32[8,128]{1,0:T(8,128)S(1)}, u32[]{:S(2)}, u32[]{:S(2)}) collective-permute-start(f32[8,128]{1,0:T(8,128)S(1)} %get-tuple-element.13), channel_id=1, source_target_pairs={{0,1},{1,2},{2,3},{3,4},{4,5},{5,6},{6,7},{7,8},{8,9},{9,10},{10,1... | collective-permute-start | bytes 12296 | tf_op jit(solution)/shard_map/ppermute | solution.py:23
  5.7 0.0 collective-permute-done.1.high_ref
  5.7 0.0 copy-start.1
  5.7 6.3 %collective-permute-done.low_ref = f32[8,128]{1,0:T(8,128)S(1)} collective-permute-done((f32[8,128]{1,0:T(8,128)S(1)}, f32[8,128]{1,0:T(8,128)S(1)}, u32[]{:S(2)}, u32[]{:S(2)}) %collective-permute-start) | collective-permute-done | bytes 4128 | tf_op jit(solution)/shard_map/ppermute | solution.py:23
  12.0 0.0 copy-start.3
  12.0 0.0 copy-done.1
  12.0 0.6 copy-done.3
  12.6 9.5 %element_images.1 = (f32[8,4096]{1,0:T(8,128)}, f32[8,128]{1,0:T(8,128)}, f32[8,128]{1,0:T(8,128)}) custom-call(f32[8,128]{1,0:T(8,128)} %copy-done.3, f32[8,4096]{1,0:T(8,128)} %probes_ref.1, f32[8,128]{1,0:T(8,128)} %copy-done.1, s32[8,2048]{1,0:T(8,128)} %connectivity_ref.1, f32[8,8,2048]{2,1,0:T(8,128)} %sensitivity_ref.1, f32[8,2048]{1,0:T(8,128)} %weight_ref.1, ...), custom_call_target="tpu_custom_call" | custom-call | tf_op jit(solution)/shard_map/element_images/pallas_call | solution.py:171
  22.1 1.9 %collective-permute-start.2 = (f32[8,128]{1,0:T(8,128)}, f32[8,128]{1,0:T(8,128)S(1)}, u32[]{:S(2)}, u32[]{:S(2)}) collective-permute-start(f32[8,128]{1,0:T(8,128)} %get-tuple-element.8), channel_id=1, source_target_pairs={{1,0},{2,1},{3,2},{4,3},{5,4},{6,5},{7,6},{8,7},{9,8},{10,9},{11,1... | collective-permute-start | bytes 12296 | tf_op jit(solution)/shard_map/ppermute | solution.py:23
  24.0 2.4 %collective-permute-start.3 = (f32[8,128]{1,0:T(8,128)}, f32[8,128]{1,0:T(8,128)S(1)}, u32[]{:S(2)}, u32[]{:S(2)}) collective-permute-start(f32[8,128]{1,0:T(8,128)} %get-tuple-element.9), channel_id=1, source_target_pairs={{0,1},{1,2},{2,3},{3,4},{4,5},{5,6},{6,7},{7,8},{8,9},{9,10},{10,1... | collective-permute-start | bytes 12296 | tf_op jit(solution)/shard_map/ppermute | solution.py:23
  26.5 0.0 collective-permute-done.2.lower_ref
  26.5 0.0 copy-start.2
  26.5 2.7 %collective-permute-done.3.upper_ref = f32[8,128]{1,0:T(8,128)S(1)} collective-permute-done((f32[8,128]{1,0:T(8,128)}, f32[8,128]{1,0:T(8,128)S(1)}, u32[]{:S(2)}, u32[]{:S(2)}) %collective-permute-start.3) | collective-permute-done | bytes 4128 | tf_op jit(solution)/shard_map/ppermute | solution.py:23
  29.2 0.0 copy-start.4
  29.2 0.0 copy-done.2
  29.2 0.6 copy-done.4
  29.8 1.6 %rims.1 = f32[8,4096]{1,0:T(8,128)} custom-call(f32[8,4096]{1,0:T(8,128)} %get-tuple-element.7.images_ref, f32[8,128]{1,0:T(8,128)} %copy-done.2, f32[8,128]{1,0:T(8,128)} %copy-done.4), custom_call_target="tpu_custom_call" | custom-call | tf_op jit(solution)/shard_map/rims/pallas_call | solution.py:429
  31.3 12.2 %all_to_all.53 = f32[8,16,256]{2,0,1:T(8,128)} all-to-all(f32[8,16,256]{2,0,1:T(8,128)} %bitcast.11), channel_id=1, replica_groups=mesh['probe'=16,'space'=32] {'probe'}, dimensions={1} | all-to-all | bytes 262144 | tf_op jit(solution)/shard_map/all_to_all | solution.py:482
  43.5 2.0 %gram.1 = f32[16,16,128]{2,1,0:T(8,128)} custom-call(f32[128,256]{1,0:T(8,128)} %bitcast.9), custom_call_target="tpu_custom_call" | custom-call | tf_op jit(solution)/shard_map/gram/pallas_call | solution.py:429
  45.5 12.2 %all_to_all.54.parts_ref = f32[16,16,128]{2,1,0:T(8,128)} all-to-all(f32[16,16,128]{2,1,0:T(8,128)} %gram.1), channel_id=1, replica_groups=mesh['probe'=16,'space'=32] {'probe'}, dimensions={0} | all-to-all | bytes 262144 | tf_op jit(solution)/shard_map/all_to_all | solution.py:449
  57.7 1.5 %probe_sum.1.own_ref = f32[16,128]{1,0:T(8,128)} custom-call(f32[16,16,128]{2,1,0:T(8,128)} %all_to_all.54.parts_ref), custom_call_target="tpu_custom_call" | custom-call | tf_op jit(solution)/shard_map/probe_sum/pallas_call | solution.py:429
  59.2 1.9 %collective-permute-start.4 = (f32[16,128]{1,0:T(8,128)}, f32[16,128]{1,0:T(8,128)S(1)}, u32[]{:S(2)}, u32[]{:S(2)}) collective-permute-start(f32[16,128]{1,0:T(8,128)} %probe_sum.1.own_ref), channel_id=1, source_target_pairs={{0,1},{1,0},{2,3},{3,2},{4,5},{5,4},{6,7},{7,6},{8,9},{9,8},{10,11... | collective-permute-start | bytes 24584 | tf_op jit(solution)/shard_map/ppermute | solution.py:451
  61.1 1.3 collective-permute-done.4.other_ref
  62.5 0.0 copy-start
  62.5 0.6 copy-done
  63.1 1.4 %core_sum.1 = f32[16,16,128]{2,1,0:T(8,128)} custom-call(f32[16,128]{1,0:T(8,128)} %probe_sum.1.own_ref, f32[16,128]{1,0:T(8,128)} %copy-done), custom_call_target="tpu_custom_call" | custom-call | tf_op jit(solution)/shard_map/core_sum/pallas_call | solution.py:429
  64.5 30.8 %all_to_all.55.parts_ref = f32[16,16,128]{2,1,0:T(8,128)} all-to-all(f32[16,16,128]{2,1,0:T(8,128)} %core_sum.1), channel_id=1, replica_groups={{0,2,4,6,8,10,12,14,16,18,20,22,24,26,28,30},{1,3,5,7,9,11,13,15,17,19,..., dimensions={0} | all-to-all | bytes 262144 | tf_op jit(solution)/shard_map/all_to_all | solution.py:454
  95.3 1.6 %space_sum.1 = f32[16,16,128]{2,1,0:T(8,128)} custom-call(f32[16,16,128]{2,1,0:T(8,128)} %all_to_all.55.parts_ref), custom_call_target="tpu_custom_call" | custom-call | tf_op jit(solution)/shard_map/space_sum/pallas_call | solution.py:429
  96.9 12.2 %all_to_all.56.pair_ref = f32[16,16,128]{2,1,0:T(8,128)} all-to-all(f32[16,16,128]{2,1,0:T(8,128)} %space_sum.1), channel_id=1, replica_groups=mesh['probe'=16,'space'=32] {'probe'}, dimensions={0} | all-to-all | bytes 262144 | tf_op jit(solution)/shard_map/all_to_all | solution.py:456
  109.0 14.9 %basis.1 = (f32[128,256]{1,0:T(8,128)}, f32[128,128]{1,0:T(8,128)}) custom-call(f32[16,16,128]{2,1,0:T(8,128)} %all_to_all.56.pair_ref, f32[128,256]{1,0:T(8,128)} %bitcast.10), custom_call_target="tpu_custom_call" | custom-call | tf_op jit(solution)/shard_map/basis/pallas_call | solution.py:429
  123.9 11.5 %all_to_all.57 = f32[16,8,256]{2,1,0:T(8,128)S(1)} all-to-all(f32[16,8,256]{2,1,0:T(8,128)} %bitcast.13), channel_id=1, replica_groups=mesh['probe'=16,'space'=32] {'probe'}, dimensions={0} | all-to-all | bytes 262144 | tf_op jit(solution)/shard_map/all_to_all | solution.py:484
  135.3 0.7 copy.8
Async XLA Ops:
  1.3 4.3 %collective-permute-start.1 = (f32[8,128]{1,0:T(8,128)S(1)}, f32[8,128]{1,0:T(8,128)S(1)}, u32[]{:S(2)}, u32[]{:S(2)}) collective-permute-start(f32[8,128]{1,0:T(8,128)S(1)} %get-tuple-element.12), channel_id=1, source_target_pairs={{1,0},{2,1},{3,2},{4,3},{5,4},{6,5},{7,6},{8,7},{9,8},{10,9},{11,1... | collective-permute-start | bytes 12296 | tf_op jit(solution)/shard_map/ppermute | solution.py:23
  3.3 8.7 %collective-permute-start = (f32[8,128]{1,0:T(8,128)S(1)}, f32[8,128]{1,0:T(8,128)S(1)}, u32[]{:S(2)}, u32[]{:S(2)}) collective-permute-start(f32[8,128]{1,0:T(8,128)S(1)} %get-tuple-element.13), channel_id=1, source_target_pairs={{0,1},{1,2},{2,3},{3,4},{4,5},{5,6},{6,7},{7,8},{8,9},{9,10},{10,1... | collective-permute-start | bytes 12296 | tf_op jit(solution)/shard_map/ppermute | solution.py:23
  5.7 6.3 %copy-start.1 = (f32[8,128]{1,0:T(8,128)}, f32[8,128]{1,0:T(8,128)S(1)}, u32[]{:S(2)}) copy-start(f32[8,128]{1,0:T(8,128)S(1)} %collective-permute-done.1.high_ref) | copy-start | bytes 12292
  12.0 0.6 copy-start.3
  22.1 4.3 %collective-permute-start.2 = (f32[8,128]{1,0:T(8,128)}, f32[8,128]{1,0:T(8,128)S(1)}, u32[]{:S(2)}, u32[]{:S(2)}) collective-permute-start(f32[8,128]{1,0:T(8,128)} %get-tuple-element.8), channel_id=1, source_target_pairs={{1,0},{2,1},{3,2},{4,3},{5,4},{6,5},{7,6},{8,7},{9,8},{10,9},{11,1... | collective-permute-start | bytes 12296 | tf_op jit(solution)/shard_map/ppermute | solution.py:23
  24.0 5.1 %collective-permute-start.3 = (f32[8,128]{1,0:T(8,128)}, f32[8,128]{1,0:T(8,128)S(1)}, u32[]{:S(2)}, u32[]{:S(2)}) collective-permute-start(f32[8,128]{1,0:T(8,128)} %get-tuple-element.9), channel_id=1, source_target_pairs={{0,1},{1,2},{2,3},{3,4},{4,5},{5,6},{6,7},{7,8},{8,9},{9,10},{10,1... | collective-permute-start | bytes 12296 | tf_op jit(solution)/shard_map/ppermute | solution.py:23
  26.5 2.7 %copy-start.2 = (f32[8,128]{1,0:T(8,128)}, f32[8,128]{1,0:T(8,128)S(1)}, u32[]{:S(2)}) copy-start(f32[8,128]{1,0:T(8,128)S(1)} %collective-permute-done.2.lower_ref) | copy-start | bytes 12292
  29.2 0.6 copy-start.4
  59.2 3.3 %collective-permute-start.4 = (f32[16,128]{1,0:T(8,128)}, f32[16,128]{1,0:T(8,128)S(1)}, u32[]{:S(2)}, u32[]{:S(2)}) collective-permute-start(f32[16,128]{1,0:T(8,128)} %probe_sum.1.own_ref), channel_id=1, source_target_pairs={{0,1},{1,0},{2,3},{3,2},{4,5},{5,4},{6,7},{7,6},{8,9},{9,8},{10,11... | collective-permute-start | bytes 24584 | tf_op jit(solution)/shard_map/ppermute | solution.py:451
  62.5 0.6 copy-start

commit v7 on v6

--- a/solution.py
+++ b/solution.py
@@ -12,6 +12,7 @@
 LANES = 128
 WIDE = 256
 CORES = 2
+GRANT = 16 * 2**20
 TOGETHER = 8
 
 highest = lax.Precision.HIGHEST
@@ -35,9 +36,15 @@
 
 
 def element_kernel(
-    low_ref, probes_ref, high_ref, connectivity_ref, sensitivity_ref, weight_ref, prior_ref,
-    images_ref, lower_ref, upper_ref, total_ref,
+    below_ref, probes_ref, above_ref, connectivity_ref, sensitivity_ref, weight_ref, prior_ref,
+    images_ref, lower_ref, upper_ref, total_ref, low_ref, high_ref, low_done, high_done,
 ):
+    low = pltpu.make_async_copy(below_ref, low_ref, low_done)
+    high = pltpu.make_async_copy(above_ref, high_ref, high_done)
+    low.start()
+    high.start()
+    low.wait()
+    high.wait()
     probe_count, node_count = probes_ref.shape
     corner_count, element_count = connectivity_ref.shape
     gauss_count = sensitivity_ref.shape[0]
@@ -167,18 +174,32 @@
     blocks = (node_count + 2 * HALO) // WIDE
     rows = (blocks + -(-blocks // 2)) * 2 * probe_count
     vmem = pl.BlockSpec(memory_space=pltpu.VMEM)
+    away = pl.BlockSpec(memory_space=pl.ANY)
     rim = jax.ShapeDtypeStruct((probe_count, HALO), jnp.float32)
     return pl.pallas_call(
         element_kernel,
         out_shape=(jax.ShapeDtypeStruct(probes.shape, jnp.float32), rim, rim),
-        in_specs=[vmem] * 7,
+        in_specs=[away, vmem, away, vmem, vmem, vmem, vmem],
         out_specs=(vmem, vmem, vmem),
-        scratch_shapes=[pltpu.VMEM((rows, WIDE), jnp.float32)],
+        scratch_shapes=[
+            pltpu.VMEM((rows, WIDE), jnp.float32),
+            pltpu.VMEM((probe_count, HALO), jnp.float32),
+            pltpu.VMEM((probe_count, HALO), jnp.float32),
+            pltpu.SemaphoreType.DMA,
+            pltpu.SemaphoreType.DMA,
+        ],
+        compiler_params=pltpu.CompilerParams(vmem_limit_bytes=GRANT),
         name="element_images",
     )(low, probes, high, connectivity, sensitivity, obs_weight, prior_weight.reshape(1, -1))
 
 
-def rim_kernel(images_ref, lower_ref, upper_ref, sum_ref):
+def rim_kernel(images_ref, low_ref, up_ref, sum_ref, lower_ref, upper_ref, low_done, up_done):
+    low = pltpu.make_async_copy(low_ref, lower_ref, low_done)
+    up = pltpu.make_async_copy(up_ref, upper_ref, up_done)
+    low.start()
+    up.start()
+    low.wait()
+    up.wait()
     node_count = images_ref.shape[1]
     sum_ref[...] = images_ref[...]
     sum_ref[:, :HALO] = images_ref[:, :HALO] + upper_ref[...]
@@ -283,7 +304,14 @@
     total_ref[...] = jnp.concatenate([high, low], axis=0)
 
 
-def spread_kernel(own_ref, other_ref, copies_ref):
+def fetched(source_ref, target_ref, semaphore):
+    copy = pltpu.make_async_copy(source_ref, target_ref, semaphore)
+    copy.start()
+    copy.wait()
+
+
+def spread_kernel(own_ref, away_ref, copies_ref, other_ref, semaphore):
+    fetched(away_ref, other_ref, semaphore)
     high, low = added(halves(own_ref[...]), halves(other_ref[...]))
     total = jnp.concatenate([high, low], axis=0)
     for k in range(copies_ref.shape[0]):
@@ -423,15 +451,18 @@
     factor_ref[...] = factor * (power_of_two(across) * (1.0 / scale))
 
 
-def in_vmem(kernel, name, out_shape, *operands, scratch=()):
+def in_vmem(kernel, name, out_shape, *operands, scratch=(), away=()):
     vmem = pl.BlockSpec(memory_space=pltpu.VMEM)
     single = not isinstance(out_shape, tuple)
     return pl.pallas_call(
         kernel,
         out_shape=out_shape,
-        in_specs=[vmem] * len(operands),
+        in_specs=[
+            pl.BlockSpec(memory_space=pl.ANY) if k in away else vmem for k in range(len(operands))
+        ],
         out_specs=vmem if single else tuple(vmem for _ in out_shape),
         scratch_shapes=scratch,
+        compiler_params=pltpu.CompilerParams(vmem_limit_bytes=GRANT),
         name=name,
     )(*operands)
 
@@ -449,7 +480,8 @@
     gram = lax.all_to_all(gram, "probe", 0, 0, tiled=True)
     own = in_vmem(sum_kernel, "probe_sum", one, gram)
     other = lax.ppermute(own, "space", [(k, k ^ 1) for k in range(places)])
-    spread = in_vmem(spread_kernel, "core_sum", copies, own, other)
+    spread = in_vmem(spread_kernel, "core_sum", copies, own, other, away=(1,),
+        scratch=(pltpu.VMEM((count, size), jnp.float32), pltpu.SemaphoreType.DMA))
     groups = [[core + CORES * k for k in range(levels)] for core in range(CORES)]
     spread = lax.all_to_all(spread, "space", 0, 0, tiled=True, axis_index_groups=groups)
     whole = in_vmem(sum_spread_kernel, "space_sum", pair, spread)
@@ -476,7 +508,8 @@
     upper_rim = shifted(upper, "space", 1)
     images = in_vmem(
         rim_kernel, "rims", jax.ShapeDtypeStruct(images.shape, jnp.float32),
-        images, lower_rim, upper_rim,
+        images, lower_rim, upper_rim, away=(1, 2),
+        scratch=(pltpu.VMEM(lower_rim.shape, jnp.float32),) * 2 + (pltpu.SemaphoreType.DMA,) * 2,
     )
     scale = math.sqrt(float(node_count * lax.axis_size("space")))
     rows = lax.all_to_all(images, "probe", 1, 0, tiled=True)

time: 137 us -> 125 us (0.912)
  Pallas kernels: 32.5 us -> 22.2 us
  blocking collectives: 78.7 us -> 75.5 us
  local copies, waits for them, and re-layouts: 3.14 us -> 4.99 us
    pallas_call x6, Pallas kernels: 23 us -> 14.4 us  [in_vmem(): pl.pallas_call(kernel, out_shape=out_shape, in_specs=[pl.BlockSpec(memory...]
    unnamed x11, local copies, waits for them, and re-layouts: 2.44 us -> 4.28 us
    pallas_call x1, Pallas kernels: 9.52 us -> 7.82 us  [element_images(): pl.pallas_call(element_kernel, out_shape=(jax.ShapeDtypeStruct(probes.sha...]
where the time goes in v7:
time: 125 us; the launch traced here: 124 us
  blocking collectives  75.5 us (60%)
  Pallas kernels  22.2 us (18%)
  starting transfers between devices  10.6 us (8%)
  waiting for transfers between devices  9.97 us (8%)
  local copies, waits for them, and re-layouts  4.99 us (4%)
    all_to_all x1, blocking collectives, orthonormal(): lax.all_to_all(spread, 'space', 0, 0, tiled=True, axis_index_groups=groups)  31.3 us
    pallas_call x6, Pallas kernels, in_vmem(): pl.pallas_call(kernel, out_shape=out_shape, in_specs=[pl.BlockSpec(memory...  14.4 us
    all_to_all x1, blocking collectives, orthonormal(): gram = lax.all_to_all(gram, 'probe', 0, 0, tiled=True)  11.1 us
    all_to_all x1, blocking collectives, orthonormal(): whole = lax.all_to_all(whole, 'probe', 0, 0, tiled=True)  11.1 us
    all_to_all x1, blocking collectives, on_device(): return (lax.all_to_all(basis, 'probe', 0, 1, tiled=True), factor)  11 us
    all_to_all x1, blocking collectives, on_device(): rows = lax.all_to_all(images, 'probe', 1, 0, tiled=True)  11 us
    ppermute x4, waiting for transfers between devices, shifted(): return lax.ppermute(block, axis, route)  8.83 us
    ppermute x4, starting transfers between devices, shifted(): return lax.ppermute(block, axis, route)  8.64 us
  transfers between devices with their start and end apart: 5, of which 3 were waited for; matrix products, arithmetic and copies ran while one was open for 0% of the time, Pallas kernels for 0%

profile of v7, /device:TPU:32, one launch (start us, length us, event | category | flops | bytes accessed | tf_op | source)
XLA Modules:
  0.0 124.0 jit_solution(10653049160633326451)
XLA Ops:
  0.6 0.0 copy-start.4
  0.6 0.7 fusion
  1.4 1.9 %collective-permute-start.1 = (f32[8,128]{1,0:T(8,128)S(1)}, f32[8,128]{1,0:T(8,128)S(1)}, u32[]{:S(2)}, u32[]{:S(2)}) collective-permute-start(f32[8,128]{1,0:T(8,128)S(1)} %get-tuple-element.12), channel_id=1, source_target_pairs={{1,0},{2,1},{3,2},{4,3},{5,4},{6,5},{7,6},{8,7},{9,8},{10,9},{11,1... | collective-permute-start | bytes 12296 | tf_op jit(solution)/shard_map/ppermute | solution.py:24
  3.3 2.4 %collective-permute-start = (f32[8,128]{1,0:T(8,128)S(1)}, f32[8,128]{1,0:T(8,128)S(1)}, u32[]{:S(2)}, u32[]{:S(2)}) collective-permute-start(f32[8,128]{1,0:T(8,128)S(1)} %get-tuple-element.13), channel_id=1, source_target_pairs={{0,1},{1,2},{2,3},{3,4},{4,5},{5,6},{6,7},{7,8},{8,9},{9,10},{10,1... | collective-permute-start | bytes 12296 | tf_op jit(solution)/shard_map/ppermute | solution.py:24
  5.7 0.0 collective-permute-done.1.above_ref
  5.7 6.3 %collective-permute-done.below_ref = f32[8,128]{1,0:T(8,128)S(1)} collective-permute-done((f32[8,128]{1,0:T(8,128)S(1)}, f32[8,128]{1,0:T(8,128)S(1)}, u32[]{:S(2)}, u32[]{:S(2)}) %collective-permute-start) | collective-permute-done | bytes 4128 | tf_op jit(solution)/shard_map/ppermute | solution.py:24
  12.0 0.0 copy-done.4
  12.0 0.0 copy-start
  12.0 1.0 copy-done
  13.1 0.0 copy-start.1
  13.1 0.9 copy-done.1
  14.0 0.0 copy-start.2
  14.0 0.8 copy-done.2
  14.8 0.0 copy-start.3
  14.8 0.8 copy-done.3
  15.6 7.8 %element_images.1 = (f32[8,4096]{1,0:T(8,128)S(1)}, f32[8,128]{1,0:T(8,128)S(1)}, f32[8,128]{1,0:T(8,128)S(1)}) custom-call(f32[8,128]{1,0:T(8,128)S(1)} %collective-permute-done.below_ref, f32[8,4096]{1,0:T(8,128)S(1)} %copy-done.1, f32[8,128]{1,0:T(8,128)S(1)} %collective-permute-done.1.above_ref, s32[8,2048]{1,0:T(8,128)S(1)} %copy-done.2, ...), custom_call_target="tpu_custom_call" | custom-call | tf_op jit(solution)/shard_map/element_images/pallas_call | solution.py:179
  23.5 1.9 %collective-permute-start.2 = (f32[8,128]{1,0:T(8,128)S(1)}, f32[8,128]{1,0:T(8,128)S(1)}, u32[]{:S(2)}, u32[]{:S(2)}) collective-permute-start(f32[8,128]{1,0:T(8,128)S(1)} %get-tuple-element.8), channel_id=1, source_target_pairs={{1,0},{2,1},{3,2},{4,3},{5,4},{6,5},{7,6},{8,7},{9,8},{10,9},{11,1... | collective-permute-start | bytes 12296 | tf_op jit(solution)/shard_map/ppermute | solution.py:24
  25.4 2.4 %collective-permute-start.3 = (f32[8,128]{1,0:T(8,128)S(1)}, f32[8,128]{1,0:T(8,128)S(1)}, u32[]{:S(2)}, u32[]{:S(2)}) collective-permute-start(f32[8,128]{1,0:T(8,128)S(1)} %get-tuple-element.9), channel_id=1, source_target_pairs={{0,1},{1,2},{2,3},{3,4},{4,5},{5,6},{6,7},{7,8},{8,9},{9,10},{10,1... | collective-permute-start | bytes 12296 | tf_op jit(solution)/shard_map/ppermute | solution.py:24
  27.8 0.0 collective-permute-done.2.low_ref
  27.8 2.5 %collective-permute-done.3.up_ref = f32[8,128]{1,0:T(8,128)S(1)} collective-permute-done((f32[8,128]{1,0:T(8,128)S(1)}, f32[8,128]{1,0:T(8,128)S(1)}, u32[]{:S(2)}, u32[]{:S(2)}) %collective-permute-start.3) | collective-permute-done | bytes 4128 | tf_op jit(solution)/shard_map/ppermute | solution.py:24
  30.4 11.0 %all_to_all.53 = f32[8,16,256]{2,0,1:T(8,128)S(1)} all-to-all(f32[8,16,256]{2,0,1:T(8,128)S(1)} %bitcast.11), channel_id=1, replica_groups=mesh['probe'=16,'space'=32] {'probe'}, dimensions={1} | all-to-all | bytes 262144 | tf_op jit(solution)/shard_map/all_to_all | solution.py:515
  41.4 0.5 gram.1
  41.9 11.1 %all_to_all.54.parts_ref = f32[16,16,128]{2,1,0:T(8,128)S(1)} all-to-all(f32[16,16,128]{2,1,0:T(8,128)S(1)} %gram.1), channel_id=1, replica_groups=mesh['probe'=16,'space'=32] {'probe'}, dimensions={0} | all-to-all | bytes 262144 | tf_op jit(solution)/shard_map/all_to_all | solution.py:480
  53.0 1.9 %collective-permute-start.4 = (f32[16,128]{1,0:T(8,128)S(1)}, f32[16,128]{1,0:T(8,128)S(1)}, u32[]{:S(2)}, u32[]{:S(2)}) collective-permute-start(f32[16,128]{1,0:T(8,128)S(1)} %probe_sum.1.own_ref), channel_id=1, source_target_pairs={{0,1},{1,0},{2,3},{3,2},{4,5},{5,4},{6,7},{7,6},{8,9},{9,8},{10,11... | collective-permute-start | bytes 24584 | tf_op jit(solution)/shard_map/ppermute | solution.py:482
  54.9 1.1 collective-permute-done.4.away_ref
  56.1 31.3 %all_to_all.55.parts_ref = f32[16,16,128]{2,1,0:T(8,128)S(1)} all-to-all(f32[16,16,128]{2,1,0:T(8,128)S(1)} %core_sum.1), channel_id=1, replica_groups={{0,2,4,6,8,10,12,14,16,18,20,22,24,26,28,30},{1,3,5,7,9,11,13,15,17,19,..., dimensions={0} | all-to-all | bytes 262144 | tf_op jit(solution)/shard_map/all_to_all | solution.py:486
  87.4 11.1 %all_to_all.56.pair_ref = f32[16,16,128]{2,1,0:T(8,128)S(1)} all-to-all(f32[16,16,128]{2,1,0:T(8,128)S(1)} %space_sum.1), channel_id=1, replica_groups=mesh['probe'=16,'space'=32] {'probe'}, dimensions={0} | all-to-all | bytes 262144 | tf_op jit(solution)/shard_map/all_to_all | solution.py:488
  98.5 13.8 %basis.1 = (f32[128,256]{1,0:T(8,128)S(1)}, f32[128,128]{1,0:T(8,128)}) custom-call(f32[16,16,128]{2,1,0:T(8,128)S(1)} %all_to_all.56.pair_ref, f32[128,256]{1,0:T(8,128)S(1)} %bitcast.10), custom_call_target="tpu_custom_call" | custom-call | tf_op jit(solution)/shard_map/basis/pallas_call | solution.py:457
  112.3 11.0 %all_to_all.57 = f32[16,8,256]{2,1,0:T(8,128)S(1)} all-to-all(f32[16,8,256]{2,1,0:T(8,128)S(1)} %bitcast.12), channel_id=1, replica_groups=mesh['probe'=16,'space'=32] {'probe'}, dimensions={0} | all-to-all | bytes 262144 | tf_op jit(solution)/shard_map/all_to_all | solution.py:517
  123.3 0.7 copy.8
  (4 shorter events, 0.2 us)
Async XLA Ops:
  0.6 11.4 %copy-start.4 = (f32[4096]{0:T(1024)S(1)}, f32[4096]{0:T(1024)}, u32[]{:S(2)}) copy-start(f32[4096]{0:T(1024)} %param.8) | copy-start | bytes 49156
  1.4 4.3 %collective-permute-start.1 = (f32[8,128]{1,0:T(8,128)S(1)}, f32[8,128]{1,0:T(8,128)S(1)}, u32[]{:S(2)}, u32[]{:S(2)}) collective-permute-start(f32[8,128]{1,0:T(8,128)S(1)} %get-tuple-element.12), channel_id=1, source_target_pairs={{1,0},{2,1},{3,2},{4,3},{5,4},{6,5},{7,6},{8,7},{9,8},{10,9},{11,1... | collective-permute-start | bytes 12296 | tf_op jit(solution)/shard_map/ppermute | solution.py:24
  3.3 8.7 %collective-permute-start = (f32[8,128]{1,0:T(8,128)S(1)}, f32[8,128]{1,0:T(8,128)S(1)}, u32[]{:S(2)}, u32[]{:S(2)}) collective-permute-start(f32[8,128]{1,0:T(8,128)S(1)} %get-tuple-element.13), channel_id=1, source_target_pairs={{0,1},{1,2},{2,3},{3,4},{4,5},{5,6},{6,7},{7,8},{8,9},{9,10},{10,1... | collective-permute-start | bytes 12296 | tf_op jit(solution)/shard_map/ppermute | solution.py:24
  12.0 1.0 copy-start
  13.1 0.9 copy-start.1
  14.0 0.8 copy-start.2
  14.8 0.8 copy-start.3
  23.5 4.3 %collective-permute-start.2 = (f32[8,128]{1,0:T(8,128)S(1)}, f32[8,128]{1,0:T(8,128)S(1)}, u32[]{:S(2)}, u32[]{:S(2)}) collective-permute-start(f32[8,128]{1,0:T(8,128)S(1)} %get-tuple-element.8), channel_id=1, source_target_pairs={{1,0},{2,1},{3,2},{4,3},{5,4},{6,5},{7,6},{8,7},{9,8},{10,9},{11,1... | collective-permute-start | bytes 12296 | tf_op jit(solution)/shard_map/ppermute | solution.py:24
  25.4 4.9 %collective-permute-start.3 = (f32[8,128]{1,0:T(8,128)S(1)}, f32[8,128]{1,0:T(8,128)S(1)}, u32[]{:S(2)}, u32[]{:S(2)}) collective-permute-start(f32[8,128]{1,0:T(8,128)S(1)} %get-tuple-element.9), channel_id=1, source_target_pairs={{0,1},{1,2},{2,3},{3,4},{4,5},{5,6},{6,7},{7,8},{8,9},{9,10},{10,1... | collective-permute-start | bytes 12296 | tf_op jit(solution)/shard_map/ppermute | solution.py:24
  53.0 3.1 %collective-permute-start.4 = (f32[16,128]{1,0:T(8,128)S(1)}, f32[16,128]{1,0:T(8,128)S(1)}, u32[]{:S(2)}, u32[]{:S(2)}) collective-permute-start(f32[16,128]{1,0:T(8,128)S(1)} %probe_sum.1.own_ref), channel_id=1, source_target_pairs={{0,1},{1,0},{2,3},{3,2},{4,5},{5,4},{6,7},{7,6},{8,9},{9,8},{10,11... | collective-permute-start | bytes 24584 | tf_op jit(solution)/shard_map/ppermute | solution.py:482
